TPU v7x, 256 devices: a whole 4x4x8 slice. The times are simulated.
256 devices in a mesh: row: 32 (over z, x), col: 8 (over y, core).
Axes of the slice: x: 4, y: 4, z: 8, core: 2. Of those that a mesh axis runs over, the one named last changes fastest.
Arguments:
- hamiltonian: float32 [16384, 16384], P('row', 'col'), may hold values from -64 to 64, as said below
Outputs:
- updated: float32 [16384, 16384], P('row', 'col')
Inputs may be any that keep to these rules, and one draw needn't show every extreme that they name: hamiltonian is symmetric as a matrix in natural order.
All inputs are finite; a program needn't handle non-finite values.
Results may differ from a plain program's by a relative error of at most 0.0001.
Values sent between devices are 32-bit elements; how exact they have to be, the bound alone decides.
A program may use at most 64 MiB of HBM per device.

v0:
```python
import jax
import jax.numpy as jnp
from jax import lax
from jax.sharding import Mesh
from jax.sharding import PartitionSpec as P

NB = 128
PANELS = 2
ROW = ("row_0", "row_1")


HIGH = lax.Precision.HIGHEST


def broadcast(shard, axis, root):
    return lax.dynamic_index_in_dim(lax.all_gather(shard, axis), root, 0, keepdims=False)


def broadcast_by_axis(shard, axes, root):
    shard = jnp.where(lax.axis_index(axes) == root, shard, jnp.zeros_like(shard))
    for axis in axes:
        shard = lax.psum(shard, axis)
    return shard


def from_everyone(shard, axis):
    copies = jnp.broadcast_to(shard, (lax.axis_size(axis), *shard.shape))
    return lax.all_to_all(copies, axis, split_axis=0, concat_axis=0, tiled=True)


def of_everyone(shard, axis):
    return from_everyone(shard, axis).sum(axis=0)


def contract(left, right, left_dim, right_dim):
    return lax.dot_general(left, right, (((left_dim,), (right_dim,)), ((), ())), precision=HIGH)


def owners_fetch(product_rows, rows_grid, cols_grid, col_index):
    width = product_rows.shape[1]
    pieces = []
    for owner in range(rows_grid // cols_grid):
        root = col_index + owner * cols_grid
        piece = broadcast(product_rows, ROW, root)
        pieces.append(piece.reshape(-1, NB, width))
    stacked = jnp.stack(pieces, axis=0).transpose(1, 0, 2, 3)
    return stacked.reshape(-1, width).T


def reduce_panel(matrix, panel, natural_rows, natural_cols, rows_grid, cols_grid, col_index):
    start = panel * NB
    col_first = panel // cols_grid * NB
    candidate = matrix[:, col_first : col_first + NB]
    panel_part = broadcast(candidate, "col", panel % cols_grid)
    row_first = panel // rows_grid * NB
    stripe = matrix[row_first : row_first + NB, :]
    stripe_part = broadcast_by_axis(stripe, ROW, panel % rows_grid)
    below_rows = jnp.where((natural_rows >= start + NB)[:, None], panel_part, jnp.float32(0.0))
    below_cols = jnp.where((natural_cols >= start + NB)[None, :], stripe_part, jnp.float32(0.0))
    gram = of_everyone(contract(below_cols, below_cols, 1, 1), "col")
    factor = jnp.linalg.cholesky(gram)
    reflect_rows = lax.linalg.triangular_solve(
        factor, below_rows, left_side=False, lower=True, transpose_a=True
    )
    reflect_cols = lax.linalg.triangular_solve(factor, below_cols, left_side=True, lower=True)
    product_rows = of_everyone(contract(matrix, reflect_cols, 1, 1), "col")
    product_cols = owners_fetch(product_rows, rows_grid, cols_grid, col_index)
    coupling = of_everyone(contract(reflect_rows, product_rows, 0, 0), ROW)
    update_rows = 2.0 * product_rows - 2.0 * contract(reflect_rows, coupling, 1, 0)
    update_cols = 2.0 * product_cols - 2.0 * contract(coupling, reflect_cols, 0, 0)
    matrix = matrix - contract(reflect_rows, update_cols, 1, 0)
    return matrix - contract(update_rows, reflect_cols, 1, 0)


def body(hamiltonian):
    rows_grid = lax.axis_size(ROW)
    cols_grid = lax.axis_size("col")
    row_index = lax.axis_index(ROW)
    col_index = lax.axis_index("col")
    local_rows, local_cols = hamiltonian.shape
    row_slot = jnp.arange(local_rows, dtype=jnp.int32)
    col_slot = jnp.arange(local_cols, dtype=jnp.int32)
    natural_rows = (row_slot // NB * rows_grid + row_index) * NB + row_slot % NB
    natural_cols = (col_slot // NB * cols_grid + col_index) * NB + col_slot % NB
    matrix = hamiltonian
    for panel in range(PANELS):
        matrix = reduce_panel(
            matrix, panel, natural_rows, natural_cols, rows_grid, cols_grid, col_index
        )
    return matrix


def solution(mesh):
    torus = Mesh(mesh.devices.reshape(8, 4, mesh.shape["col"]), ("row_0", "row_1", "col"))
    return jax.shard_map(
        body,
        mesh=torus,
        in_specs=(P(ROW, "col"),),
        out_specs=P(ROW, "col"),
        check_vma=False,
    )
```

profile of v0, /device:TPU:1, one launch (start us, length us, event | category | flops | bytes accessed | tf_op | source)
XLA Modules:
  0.0 683.3 jit_solution(2036827324426908332)
XLA Ops:
  7.4 2.3 slice_select_fusion.1
  9.7 76.2 %all-reduce.5.cloned.1.call-done = f32[128,2048]{1,0:T(8,128)} async-done(((f32[128,2048]{1,0:T(8,128)}), f32[128,2048]{1,0:T(8,128)}) %all-reduce.5.cloned.1.call-update) | async-done | bytes 1048592 | tf_op jit(solution)/shard_map/psum | solution.py:22
  86.0 1.7 slice.23
  87.8 52.8 %all-reduce.7.cloned.1.call-done = f32[128,2048]{1,0:T(8,128)} async-done(((f32[128,2048]{1,0:T(8,128)}), f32[128,2048]{1,0:T(8,128)}) %all-reduce.7.cloned.1.call-update) | async-done | bytes 1048592 | tf_op jit(solution)/shard_map/psum | solution.py:22
  140.6 2.7 fusion.10
  143.3 15.9 %all_to_all.30 = f32[8,128,128]{2,1,0:T(8,128)S(1)} all-to-all(f32[8,128,128]{2,1,0:T(8,128)S(1)} %broadcast_in_dim.58), channel_id=1, replica_groups=mesh['row_0'=8,'row_1'=4,'col'=8] {'col'}, dimensions={0} | all-to-all | bytes 1048576 | tf_op jit(solution)/shard_map/all_to_all | solution.py:28
  159.3 11.7 %cholesky.44 = f32[128,128]{1,0:T(8,128)S(1)} custom-call(f32[128,128]{1,0:T(8,128)S(1)} %fusion.31), custom_call_target="Cholesky" | custom-call | tf_op jit(solution)/shard_map/jit(cholesky)/cholesky | solution.py:61
  171.1 0.7 compare_reduce_fusion.1
  171.8 0.7 fusion.24
  172.5 9.8 %custom-call.10 = f32[1,128,128]{1,2,0:T(8,128)S(1)} custom-call(f32[1,128,128]{2,1,0:T(8,128)S(1)} %fusion.24), custom_call_target="InvertDiagBlocksLowerTriangular" | custom-call | tf_op jit(solution)/shard_map/triangular_solve/custom-call.0 | solution.py:62
  182.3 1.0 fusion.8
  183.4 6.6 convolution_bitcast_fusion
  190.2 29.7 %all_to_all.31 = f32[8,512,128]{2,1,0:T(8,128)S(1)} all-to-all(f32[8,512,128]{2,1,0:T(8,128)S(1)} %broadcast_in_dim.61), channel_id=1, replica_groups=mesh['row_0'=8,'row_1'=4,'col'=8] {'col'}, dimensions={0} | all-to-all | bytes 4194304 | tf_op jit(solution)/shard_map/all_to_all | solution.py:28
  219.9 0.8 reduce_sum.55
  220.8 1.5 convolution_bitcast_fusion.2
  223.0 1.3 fusion.60
  224.3 1.6 broadcast_in_dim.62
  225.9 9.4 %all-to-all-start.2 = ((f32[32,128,128]{2,1,0:T(8,128)}), f32[32,128,128]{2,1,0:T(8,128)S(1)}, u32[]{:S(2)}, u32[]{:S(2)}) async-start(f32[32,128,128]{2,1,0:T(8,128)} %broadcast_in_dim.62), calls=%async_computation.2 | async-start | bytes 4194304 | tf_op jit(solution)/shard_map/all_to_all | solution.py:28
  235.3 56.5 %all-to-all-done.2 = f32[32,128,128]{2,1,0:T(8,128)S(1)} async-done(((f32[32,128,128]{2,1,0:T(8,128)}), f32[32,128,128]{2,1,0:T(8,128)S(1)}, u32[]{:S(2)}, u32[]{:S(2)}) %all-to-all-start.2) | async-done | bytes 2097184 | tf_op jit(solution)/shard_map/all_to_all | solution.py:28
  292.0 2.2 fusion.3
  294.2 40.5 %all-gather.11.cloned.1.call-done = f32[16384,128]{1,0:T(8,128)} async-done(((f32[512,128]{1,0:T(8,128)}), f32[16384,128]{1,0:T(8,128)}) %all-gather.11.cloned.1.call-update) | async-done | bytes 8388624 | tf_op jit(solution)/shard_map/all_gather | solution.py:16
  334.7 1.3 constant_dynamic-slice_fusion.7
  336.4 1.1 fusion.1
  337.5 3.6 fusion.61
  341.1 4.0 subtract_subtract_fusion.1
  345.2 2.0 copy-done
  347.2 1.1 slice_select_fusion
  348.3 69.6 %all-reduce.9.cloned.1.call-done = f32[128,2048]{1,0:T(8,128)} async-done(((f32[128,2048]{1,0:T(8,128)}), f32[128,2048]{1,0:T(8,128)}) %all-reduce.9.cloned.1.call-update) | async-done | bytes 1048592 | tf_op jit(solution)/shard_map/psum | solution.py:22
  418.0 1.7 slice.30
  419.8 52.6 %all-reduce.11.cloned.1.call-done = f32[128,2048]{1,0:T(8,128)} async-done(((f32[128,2048]{1,0:T(8,128)}), f32[128,2048]{1,0:T(8,128)}) %all-reduce.11.cloned.1.call-update) | async-done | bytes 1048592 | tf_op jit(solution)/shard_map/psum | solution.py:22
  472.4 2.7 fusion.6
  475.1 16.1 %all_to_all.32 = f32[8,128,128]{2,1,0:T(8,128)S(1)} all-to-all(f32[8,128,128]{2,1,0:T(8,128)S(1)} %broadcast_in_dim.64), channel_id=1, replica_groups=mesh['row_0'=8,'row_1'=4,'col'=8] {'col'}, dimensions={0} | all-to-all | bytes 1048576 | tf_op jit(solution)/shard_map/all_to_all | solution.py:28
  491.4 11.7 %cholesky.55 = f32[128,128]{1,0:T(8,128)S(1)} custom-call(f32[128,128]{1,0:T(8,128)S(1)} %fusion.28), custom_call_target="Cholesky" | custom-call | tf_op jit(solution)/shard_map/jit(cholesky)/cholesky | solution.py:61
  503.1 0.7 compare_reduce_fusion
  504.5 9.8 %custom-call.12 = f32[1,128,128]{1,2,0:T(8,128)S(1)} custom-call(f32[1,128,128]{2,1,0:T(8,128)S(1)} %fusion.25), custom_call_target="InvertDiagBlocksLowerTriangular" | custom-call | tf_op jit(solution)/shard_map/triangular_solve/custom-call.0 | solution.py:62
  514.4 1.0 fusion.4
  515.4 5.2 fusion.62
  520.8 29.7 %all_to_all.33 = f32[8,512,128]{2,1,0:T(8,128)S(1)} all-to-all(f32[8,512,128]{2,1,0:T(8,128)S(1)} %broadcast_in_dim.66), channel_id=1, replica_groups=mesh['row_0'=8,'row_1'=4,'col'=8] {'col'}, dimensions={0} | all-to-all | bytes 4194304 | tf_op jit(solution)/shard_map/all_to_all | solution.py:28
  550.4 0.8 reduce_sum.58
  551.3 1.5 convolution_bitcast_fusion.1
  553.5 1.3 fusion.63
  555.1 69.9 %all_to_all.34 = f32[32,128,128]{2,1,0:T(8,128)S(1)} all-to-all(f32[32,128,128]{2,1,0:T(8,128)S(1)} %broadcast_in_dim.67), channel_id=1, replica_groups=mesh['row_0'=8,'row_1'=4,'col'=8] {'row_0','row_1'}, dimensions={0} | all-to-all | bytes 4194304 | tf_op jit(solution)/shard_map/all_to_all | solution.py:28
  625.1 2.2 fusion.2
  627.4 36.3 %all-gather.15.cloned.1.call-done = f32[16384,128]{1,0:T(8,128)} async-done(((f32[512,128]{1,0:T(8,128)}), f32[16384,128]{1,0:T(8,128)}) %all-gather.15.cloned.1.call-update) | async-done | bytes 8388624 | tf_op jit(solution)/shard_map/all_gather | solution.py:16
  663.6 1.3 constant_dynamic-slice_fusion.3
  665.4 1.1 fusion
  666.5 3.6 fusion.64
  670.1 5.4 subtract_subtract_fusion
  (68 shorter events, 4.8 us)
Async XLA Ops:
  7.4 78.6 %all-reduce.5.cloned.1.call-start = ((), (), s32[]{:S(2)}) async-start(), calls=%async_computation.6 | async-start | bytes 2097152 | tf_op jit(solution)/shard_map/psum | solution.py:22
  9.7 130.9 %all-reduce.7.cloned.1.call-start = ((), (), s32[]{:S(2)}) async-start(), calls=%async_computation.7 | async-start | bytes 2097152 | tf_op jit(solution)/shard_map/psum | solution.py:22
  86.0 134.8 %all-gather.9.cloned.1.call-start = ((), (), s32[]{:S(2)}) async-start(), calls=%async_computation.10 | async-start | bytes 2359296 | tf_op jit(solution)/shard_map/all_gather | solution.py:16
  87.7 247.0 %all-gather.11.cloned.1.call-start = ((), (), s32[]{:S(2)}) async-start(), calls=%async_computation.11 | async-start | bytes 8650752 | tf_op jit(solution)/shard_map/all_gather | solution.py:16
  140.6 41.7 %copy-start.3 = (f32[128,2048]{1,0:T(8,128)S(1)}, f32[128,2048]{1,0:T(8,128)}, u32[]{:S(2)}) copy-start(f32[128,2048]{1,0:T(8,128)} %all-reduce.7.cloned.1.call-done) | copy-start | bytes 3145732
  222.3 0.7 copy-start.7
  224.3 67.7 %copy-start.5 = (f32[512,128]{1,0:T(8,128)S(1)}, f32[512,128]{1,0:T(8,128)}, u32[]{:S(2)}) copy-start(f32[512,128]{1,0:T(8,128)} %reduce_sum.55) | copy-start | bytes 786436
  225.9 66.0 %all-to-all-start.2 = ((f32[32,128,128]{2,1,0:T(8,128)}), f32[32,128,128]{2,1,0:T(8,128)S(1)}, u32[]{:S(2)}, u32[]{:S(2)}) async-start(f32[32,128,128]{2,1,0:T(8,128)} %broadcast_in_dim.62), calls=%async_computation.2 | async-start | bytes 4194304 | tf_op jit(solution)/shard_map/all_to_all | solution.py:28
  235.3 182.6 %all-reduce.9.cloned.1.call-start = ((), (), s32[]{:S(2)}) async-start(), calls=%async_computation.8 | async-start | bytes 2097152 | tf_op jit(solution)/shard_map/psum | solution.py:22
  336.0 1.6 copy-start.8
  336.4 4.7 copy-start.2
  336.4 4.7 copy-start.12
  345.2 2.0 copy-start
  348.3 124.1 %all-reduce.11.cloned.1.call-start = ((), (), s32[]{:S(2)}) async-start(), calls=%async_computation.9 | async-start | bytes 2097152 | tf_op jit(solution)/shard_map/psum | solution.py:22
  417.9 133.4 %all-gather.13.cloned.1.call-start = ((), (), s32[]{:S(2)}) async-start(), calls=%async_computation.12 | async-start | bytes 2359296 | tf_op jit(solution)/shard_map/all_gather | solution.py:16
  419.7 243.9 %all-gather.15.cloned.1.call-start = ((), (), s32[]{:S(2)}) async-start(), calls=%async_computation.13 | async-start | bytes 8650752 | tf_op jit(solution)/shard_map/all_gather | solution.py:16
  472.4 41.9 %copy-start.4 = (f32[128,2048]{1,0:T(8,128)S(1)}, f32[128,2048]{1,0:T(8,128)}, u32[]{:S(2)}) copy-start(f32[128,2048]{1,0:T(8,128)} %all-reduce.11.cloned.1.call-done) | copy-start | bytes 3145732
  552.8 0.7 copy-start.9
  554.9 70.3 %copy-start.6 = (f32[512,128]{1,0:T(8,128)S(1)}, f32[512,128]{1,0:T(8,128)}, u32[]{:S(2)}) copy-start(f32[512,128]{1,0:T(8,128)} %reduce_sum.58) | copy-start | bytes 786436
  664.9 1.6 copy-start.10
  665.3 4.7 copy-start.1
  665.4 4.7 copy-start.11
Sparse Core Ops, SparseCore 0:
  10.5 75.3 all-reduce.4
  88.3 52.2 all-reduce.6
  348.4 69.4 all-reduce.8
  420.1 52.2 all-reduce.10
Sparse Core Ops, SparseCore 1:
  88.3 31.0 all-gather.8
  220.8 113.8 all-gather.10
  420.3 31.0 all-gather.12
  551.4 112.2 all-gather.14
where the time goes:
time: 693 us; the launch traced here: 683 us
  waiting for transfers between devices  385 us (56%)
  blocking collectives  161 us (23%)
  other arithmetic  51.5 us (7%)
  matrix products  48.1 us (7%)
  between operations  15.8 us (2%)
  local copies, waits for them, and re-layouts  12.4 us (2%)
  starting transfers between devices  9.69 us (1%)
    psum x4, waiting for transfers between devices, broadcast_by_axis(): shard = lax.psum(shard, axis)  251 us
    all_to_all x5, blocking collectives, from_everyone(): return lax.all_to_all(copies, axis, split_axis=0, concat_axis=0, tiled=True)  161 us
    all_gather x4, waiting for transfers between devices, broadcast(): lax.all_gather(shard, axis)  76.8 us
    all_to_all x1, waiting for transfers between devices, from_everyone(): return lax.all_to_all(copies, axis, split_axis=0, concat_axis=0, tiled=True)  56.5 us
    dot_general x14, matrix products, contract(): lax.dot_general(left, right, (((left_dim,), (right_dim,)), ((), ())), pre...  43.1 us
    another operation x6, other arithmetic, reduce_panel(): factor = jnp.linalg.cholesky(gram)  24.9 us
    another operation x4, other arithmetic, reduce_panel(): lax.linalg.triangular_solve(factor, below_rows, left_side=False, lower=Tr...  21 us
  transfers between devices with their start and end apart: 9, of which 7 were waited for; matrix products, arithmetic and copies ran while one was open for 12% of the time, Pallas kernels for 0%

commit v1 on v0

v1 whole, which is shorter than its diff:
```python
import functools

import jax
import jax.numpy as jnp
from jax import lax
from jax.experimental import pallas as pl
from jax.experimental.pallas import tpu as pltpu
from jax.sharding import PartitionSpec as P

NB = 128
Z, X, C = 8, 4, 8
SH = 64
MESH = pl.DeviceIdType.MESH
HIGH = lax.Precision.HIGHEST
F32 = jnp.float32


def dot(a, b):
    return lax.dot_general(a, b, (((1,), (0,)), ((), ())), precision=HIGH, preferred_element_type=F32)


def dot_nt(a, b):
    return lax.dot_general(a, b, (((1,), (1,)), ((), ())), precision=HIGH, preferred_element_type=F32)


def sweep_steps(a, groups):
    lane = lax.broadcasted_iota(jnp.int32, (NB, NB), 1)
    sub = lax.broadcasted_iota(jnp.int32, (NB, NB), 0)
    lane_row = lax.broadcasted_iota(jnp.int32, (1, NB), 1)

    def group(_, a):
        for t in range(8):
            pivot = 1.0 / a[t : t + 1, t : t + 1]
            row = a[t : t + 1, :] * pivot
            row = jnp.where(lane_row == t, pivot, row)
            column = jnp.broadcast_to(a[:, t : t + 1], (NB, NB))
            column = jnp.where(sub == t, -1.0, column)
            a = jnp.where((lane == t) | (sub == t), 0.0, a) - column * row
        a = pltpu.roll(a, NB - 8, 0)
        return pltpu.roll(a, NB - 8, 1)

    return lax.fori_loop(0, groups, group, a)


def kernel(
    h_hbm, lhs_ref, rhs_ref,
    hv, sh, col_form, row_form, part, rsb, ysh, p2c, stack, gsum, eb, gram, inv, sc1, sc2,
    h_sem, loc_sem, sc_send, sc_recv, ra_send, ra_recv, sp_send, sp_recv,
    rp_send, rp_recv, rs_send, rs_recv, es_send, es_recv, ea_send, ea_recv,
):
    r = lax.axis_index("row")
    c = lax.axis_index("col")
    z = r // X
    x = lax.rem(r, X)
    plane = lax.rem(r, C)
    rel = lax.rem(c - plane + C, C)
    z_up = lax.rem(z + 1, Z)
    z_down = lax.rem(z + Z - 1, Z)
    z_to = jnp.where(rel < 4, z_up, z)
    half = c // 4
    same = lax.rem(z, 2) == half
    z_from = jnp.where(same, z, z_down)

    def remote(src, dst, send, recv, row, col):
        return pltpu.make_async_remote_copy(
            src_ref=src, dst_ref=dst, send_sem=send, recv_sem=recv,
            device_id=(row, col), device_id_type=MESH,
        )

    def other(d):
        return lax.rem(c + d, C)

    started = []

    def go(copy):
        copy.start()
        started.append(copy)

    copy_h = pltpu.make_async_copy(h_hbm, hv, h_sem)
    copy_h.start()

    barrier = pltpu.get_barrier_semaphore()

    def greet(row, col):
        pl.semaphore_signal(barrier, inc=1, device_id=(row, col), device_id_type=MESH)

    for d in range(1, C):
        greet(r, other(d))
    for i in range(4):
        greet(z_to * X + i, plane)
        greet(z_from * X + lax.rem(c, X), lax.rem(c + jnp.where(same, 4, 0) + i, C))
    greet(z_up * X + x, c)
    greet(z_down * X + x, c)
    pl.semaphore_wait(barrier, 17)

    def mine(ref):
        return ref.at[pl.ds(pl.multiple_of(SH * c, SH), SH)]

    def scatter(v):
        def from_root(d):
            rows = pl.ds(pl.multiple_of(SH * other(d), SH), SH)
            return remote(h_hbm.at[rows, 0:NB], sh.at[v], sc_send.at[v, d], sc_recv.at[v], r, other(d))

        def own():
            rows = pl.ds(pl.multiple_of(SH * c, SH), SH)
            return pltpu.make_async_copy(h_hbm.at[rows, 0:NB], sh.at[v], loc_sem.at[v])

        @pl.when(c == v)
        def _():
            own().start()
            for d in range(1, C):
                from_root(d).start()

        def finish():
            @pl.when(c == v)
            def _():
                own().wait()
                for d in range(1, C):
                    from_root(d).wait_send()

            @pl.when(c != v)
            def _():
                from_root(1).wait_recv()

        return finish

    my_off = pl.multiple_of(((c // 2) * 4 + r // C) * NB + lax.rem(c, 2) * SH, SH)

    def distribute(v, shard):
        def send_rows():
            for d in range(1, C):
                go(remote(shard, mine(row_form.at[v]), ra_send.at[v, d], ra_recv.at[v, c], r, other(d)))
            row_form[v, pl.ds(pl.multiple_of(SH * c, SH), SH), :] = shard[...]

        for i in range(X):
            to = lax.rem(x + i, X)
            go(remote(
                shard, col_form.at[v, pl.ds(my_off, SH)],
                sp_send.at[v, i], sp_recv.at[v, lax.rem(rel, 4)], z_to * X + to, plane,
            ))
        send_rows()

    def wait_rows(v):
        for d in range(1, C):
            rows = pl.ds(pl.multiple_of(SH * other(d), SH), SH)
            remote(row_form.at[v, rows], row_form.at[v, rows], ra_send.at[v, d], ra_recv.at[v, other(d)], r, other(d)).wait_recv()

    def piece(v, block, i):
        aligned = lax.rem(block, 2) == half
        source = jnp.where(aligned, block, lax.rem(block + Z - 1, Z))
        sender = lax.rem(c + jnp.where(aligned, 4, 0) + i, C)
        off = ((sender // 2) * 4 + source // 2) * NB + lax.rem(sender, 2) * SH
        return col_form.at[v, pl.ds(pl.multiple_of(off, SH), SH)]

    def pieces(s, up):
        if s < 4:
            return range(4)
        return range(0, 2) if up else range(2, 4)

    def ring_copy(v, s, i, up, block):
        k = 0 if up else 1
        to = z_up if up else z_down
        ref = piece(v, block, i)
        return remote(ref, ref, rp_send.at[v, k, s - 1, i], rp_recv.at[v, k, s - 1, i], to * X + x, c)

    def ring_wait_piece(v, s, i, up):
        if s == 0:
            ref = piece(v, z, i)
            remote(ref, ref, sp_send.at[v, 0], sp_recv.at[v, i], r, c).wait_recv()
            return
        block = lax.rem(z - s + Z, Z) if up else lax.rem(z + s, Z)
        ring_copy(v, s, i, up, block).wait_recv()

    def ring(v, s):
        for i in range(4):
            if s == 1:
                ring_wait_piece(v, 0, i, True)
            for up in (True, False):
                if i not in pieces(s, up):
                    continue
                if s > 1:
                    ring_wait_piece(v, s - 1, i, up)
                block = lax.rem(z - (s - 1) + Z, Z) if up else lax.rem(z + s - 1, Z)
                go(ring_copy(v, s, i, up, block))

    def ring_end(v):
        for up in (True, False):
            for i in range(4):
                if i not in pieces(4, up):
                    ring_wait_piece(v, 3, i, up)
            for i in pieces(4, up):
                ring_wait_piece(v, 4, i, up)

    def reduce_start(q):
        for d in range(1, C):
            rows = pl.ds(pl.multiple_of(SH * other(d), SH), SH)
            go(remote(part.at[q, rows], rsb.at[q, d - 1], rs_send.at[q, d], rs_recv.at[q, d], r, other(d)))

    def reduce_end(q):
        total = part[q, pl.ds(pl.multiple_of(SH * c, SH), SH), :]
        for d in range(1, C):
            remote(rsb.at[q, d - 1], rsb.at[q, d - 1], rs_send.at[q, d], rs_recv.at[q, d], r, other(d)).wait_recv()
            total = total + rsb[q, d - 1]
        return total

    def exchange_start(e, rows):
        m = rows // C
        for d in range(1, C):
            src = stack.at[e, pl.ds(pl.multiple_of(m * other(d), 8), m)]
            go(remote(src, eb.at[e, d - 1, pl.ds(0, m)], es_send.at[e, d], es_recv.at[e, d], r, other(d)))

    def exchange_mid(e, rows):
        m = rows // C
        own = pl.ds(pl.multiple_of(m * c, 8), m)
        total = stack[e, own, :]
        for d in range(1, C):
            dst = eb.at[e, d - 1, pl.ds(0, m)]
            remote(dst, dst, es_send.at[e, d], es_recv.at[e, d], r, other(d)).wait_recv()
            total = total + eb[e, d - 1, pl.ds(0, m), :]
        gsum[e, own, :] = total
        for d in range(1, C):
            ref = gsum.at[e, own]
            go(remote(ref, ref, ea_send.at[e, d], ea_recv.at[e, c], r, other(d)))

    def exchange_end(e, rows):
        m = rows // C
        for d in range(1, C):
            ref = gsum.at[e, pl.ds(pl.multiple_of(m * other(d), 8), m)]
            remote(ref, ref, ea_send.at[e, d], ea_recv.at[e, other(d)], r, other(d)).wait_recv()

    def times_h(q, src):
        @pl.loop(0, 4)
        def _(j):
            rows = pl.ds(pl.multiple_of(j * NB, NB), NB)
            part[q, rows, :] = dot(hv[rows, :], src[...])

    def transpose_to(slot, src):
        @pl.loop(0, 16)
        def _(k):
            cols = pl.ds(pl.multiple_of(k * NB, NB), NB)
            rhs_ref[slot * NB : (slot + 1) * NB, cols] = src[cols, :].T

    eye = lax.broadcasted_iota(jnp.int32, (NB, NB), 0) == lax.broadcasted_iota(jnp.int32, (NB, NB), 1)

    def scaled(q):
        diagonal = jnp.where(eye, gram[q], 0.0)
        sc1[q] = jnp.broadcast_to(lax.rsqrt(jnp.sum(diagonal, axis=0, keepdims=True)), (NB, NB))
        sc2[q] = jnp.broadcast_to(lax.rsqrt(jnp.sum(diagonal, axis=1, keepdims=True)), (NB, NB))
        inv[q] = gram[q] * sc1[q] * sc2[q]

    def sweep(q, groups):
        inv[q] = sweep_steps(inv[q], groups)

    PV, CV, YV, UV = 0, 1, 2, 3
    finish_p = scatter(PV)
    finish_c = scatter(CV)
    finish_p()

    @pl.when((r == 0) & (c < 2))
    def _():
        sh[PV] = jnp.zeros((SH, NB), F32)

    distribute(PV, sh.at[PV])
    finish_c()
    distribute(CV, sh.at[CV])
    for s in range(1, 5):
        ring(PV, s)
    ring_end(PV)
    ring(CV, 1)
    copy_h.wait()
    times_h(0, col_form.at[PV])
    reduce_start(0)
    ring(CV, 2)
    transpose_to(1, col_form.at[PV])
    stack[0, 0:NB, :] = dot(rhs_ref[NB : 2 * NB, :], col_form[PV])
    stack[0, NB : 2 * NB, :] = jnp.where(c == 1, col_form[PV, 0:NB, :], 0.0)
    exchange_start(0, 2 * NB)
    ysh[0] = reduce_end(0)
    distribute(YV, ysh.at[0])
    exchange_mid(0, 2 * NB)
    ring(CV, 3)
    ring(YV, 1)
    exchange_end(0, 2 * NB)
    gram[0] = gsum[0, 0:NB, :]
    scaled(0)
    sweep(0, 5)
    ring(CV, 4)
    ring(YV, 2)
    sweep(0, 5)
    ring(YV, 3)
    sweep(0, 6)
    ring(YV, 4)
    ring_end(CV)
    wait_rows(PV)
    wait_rows(CV)
    wait_rows(YV)
    ring_end(YV)
    transpose_to(0, col_form.at[YV])
    stack[1, 0:NB, :] = dot(rhs_ref[NB : 2 * NB, :], col_form[YV])
    stack[1, NB : 2 * NB, :] = jnp.where(c == 1, col_form[YV, 0:NB, :], 0.0)
    exchange_start(1, 2 * NB)
    exchange_mid(1, 2 * NB)
    exchange_end(1, 2 * NB)
    k1, d1, e1 = inv[0], sc1[0], sc2[0]
    s1 = gsum[1, 0:NB, :] * d1 * e1

    def factors(p, y, k, s, d):
        pk = dot(p * d[0:1, :], k)
        alpha = -2.0 * pk * d[0:1, :]
        beta = dot(4.0 * dot(pk, s) - 2.0 * (y * d[0:1, :]), k) * d[0:1, :]
        return alpha, beta

    alpha_b, beta_b = factors(gsum[0, NB : 2 * NB, :], gsum[1, NB : 2 * NB, :], k1, s1, d1)
    sub = lax.broadcasted_iota(jnp.int32, (NB, NB), 0)

    @pl.loop(0, 16)
    def _(k):
        rows = pl.ds(pl.multiple_of(k * NB, NB), NB)
        value = (
            col_form[CV, rows, :]
            + dot_nt(col_form[YV, rows, :], alpha_b)
            + dot_nt(col_form[PV, rows, :], beta_b)
        )
        p2c[rows, :] = jnp.where((k == 0) & (c < 2), 0.0, value)

    times_h(1, p2c)
    reduce_start(1)
    transpose_to(3, p2c)
    stack[2, 0:NB, :] = dot(rhs_ref[3 * NB : 4 * NB, :], p2c[...])
    stack[2, NB : 2 * NB, :] = dot(rhs_ref[0:NB, :], p2c[...])
    stack[2, 2 * NB : 3 * NB, :] = dot(rhs_ref[NB : 2 * NB, :], p2c[...])
    exchange_start(2, 3 * NB)
    ysh[1] = reduce_end(1)
    distribute(UV, ysh.at[1])
    exchange_mid(2, 3 * NB)
    ring(UV, 1)
    exchange_end(2, 3 * NB)
    gram[1] = gsum[2, 0:NB, :]
    scaled(1)
    sweep(1, 5)
    ring(UV, 2)
    sweep(1, 5)
    ring(UV, 3)
    sweep(1, 6)
    ring(UV, 4)
    t1, t2 = gsum[2, NB : 2 * NB, :], gsum[2, 2 * NB : 3 * NB, :]
    kt2 = dot(k1, t2 * e1)
    a = -2.0 * kt2 * e1
    b = dot(k1, 4.0 * dot(s1, kt2) - 2.0 * (t1 * e1)) * e1
    wait_rows(UV)
    ring_end(UV)
    transpose_to(2, col_form.at[UV])
    stack[3, 0:NB, :] = dot(rhs_ref[3 * NB : 4 * NB, :], col_form[UV])
    exchange_start(3, NB)
    exchange_mid(3, NB)
    exchange_end(3, NB)
    k2, d2, e2 = inv[1], sc1[1], sc2[1]

    def dot_tn(left, right):
        return lax.dot_general(left, right, (((0,), (0,)), ((), ())), precision=HIGH, preferred_element_type=F32)

    s2 = (gsum[3, 0:NB, :] + dot_tn(t1, a) + dot_tn(t2, b)) * d2 * e2
    for j in range(4):
        rows = slice(j * NB, (j + 1) * NB)
        p1, c1, y1, u = (row_form[v, rows, :] for v in range(4))
        alpha1, beta1 = factors(p1, y1, k1, s1, d1)
        p2 = c1 + dot_nt(y1, alpha_b) + dot_nt(p1, beta_b)
        if j == 0:
            p2 = jnp.where(r < 2, 0.0, p2)
        y2 = u + dot(y1, a) + dot(p1, b)
        alpha2, beta2 = factors(p2, y2, k2, s2, d2)
        lhs_ref[rows, 0:NB] = alpha1 + dot_nt(alpha2, a)
        lhs_ref[rows, NB : 2 * NB] = beta1 + dot_nt(alpha2, b)
        lhs_ref[rows, 2 * NB : 3 * NB] = alpha2
        lhs_ref[rows, 3 * NB : 4 * NB] = beta2
    for copy in started:
        copy.wait_send()


def factors_kernel(hamiltonian):
    rows, cols = hamiltonian.shape
    dma = pltpu.SemaphoreType.DMA
    vmem = pl.BlockSpec(memory_space=pltpu.VMEM)
    return pl.pallas_call(
        kernel,
        out_shape=(
            jax.ShapeDtypeStruct((rows, 4 * NB), F32),
            jax.ShapeDtypeStruct((4 * NB, cols), F32),
        ),
        in_specs=[pl.BlockSpec(memory_space=pl.ANY)],
        out_specs=(vmem, vmem),
        scratch_shapes=[
            pltpu.VMEM((rows, cols), F32),
            pltpu.VMEM((2, SH, NB), F32),
            pltpu.VMEM((4, cols, NB), F32),
            pltpu.VMEM((4, rows, NB), F32),
            pltpu.VMEM((2, rows, NB), F32),
            pltpu.VMEM((2, C - 1, SH, NB), F32),
            pltpu.VMEM((2, SH, NB), F32),
            pltpu.VMEM((cols, NB), F32),
            pltpu.VMEM((4, 3 * NB, NB), F32),
            pltpu.VMEM((4, 3 * NB, NB), F32),
            pltpu.VMEM((4, C - 1, 3 * NB // C, NB), F32),
            pltpu.VMEM((2, NB, NB), F32),
            pltpu.VMEM((2, NB, NB), F32),
            pltpu.VMEM((2, NB, NB), F32),
            pltpu.VMEM((2, NB, NB), F32),
            dma, dma((2,)), dma((2, C)), dma((2,)),
            dma((4, C)), dma((4, C)), dma((4, 4)), dma((4, 4)),
            dma((4, 2, 4, 4)), dma((4, 2, 4, 4)),
            dma((2, C)), dma((2, C)),
            dma((4, C)), dma((4, C)), dma((4, C)), dma((4, C)),
        ],
        compiler_params=pltpu.CompilerParams(
            collective_id=0, has_side_effects=True, vmem_limit_bytes=60 * 1024 * 1024
        ),
        name="reflector_factors",
    )(hamiltonian)


def update_kernel(h_ref, lhs_ref, rhs_ref, out_ref):
    out_ref[...] = h_ref[...] + dot(lhs_ref[...], rhs_ref[...])


def update(hamiltonian, lhs, rhs):
    rows, cols = hamiltonian.shape
    tile = 128
    return pl.pallas_call(
        update_kernel,
        grid=(rows // tile,),
        out_shape=jax.ShapeDtypeStruct((rows, cols), F32),
        in_specs=[
            pl.BlockSpec((tile, cols), lambda i: (i, 0)),
            pl.BlockSpec((tile, 4 * NB), lambda i: (i, 0)),
            pl.BlockSpec((4 * NB, cols), lambda i: (0, 0)),
        ],
        out_specs=pl.BlockSpec((tile, cols), lambda i: (i, 0)),
        compiler_params=pltpu.CompilerParams(vmem_limit_bytes=40 * 1024 * 1024),
        name="apply_factors",
    )(hamiltonian, lhs, rhs)


def body(hamiltonian):
    lhs, rhs = factors_kernel(hamiltonian)
    return update(hamiltonian, lhs, rhs)


def solution(mesh):
    return jax.shard_map(
        body, mesh=mesh, in_specs=(P("row", "col"),), out_specs=P("row", "col"), check_vma=False
    )
```

time: 693 us -> 167 us (0.24); the launches traced: 683 us -> 167 us
  waiting for transfers between devices: 385 us -> 0 us
  Pallas kernels: 0 us -> 161 us
  blocking collectives: 161 us -> 0 us
  other arithmetic: 51.5 us -> 0 us
  matrix products: 48.1 us -> 0 us
  between operations: 15.8 us -> 0.02 us
  starting transfers between devices: 9.69 us -> 0 us
    psum x4 -> x0, waiting for transfers between devices: 251 us -> none  [broadcast_by_axis(): shard = lax.psum(shard, axis)]
    pallas_call x0 -> x2, Pallas kernels: none -> 161 us  [the longest x1 152 us: factors_kernel(): pl.pallas_call(kernel, out_shape=(jax.ShapeDtypeStruct((rows, 4 * NB), F3...]
    all_to_all x5 -> x0, blocking collectives: 161 us -> none  [from_everyone(): return lax.all_to_all(copies, axis, split_axis=0, concat_axis=0, tiled=True)]
    all_gather x4 -> x0, waiting for transfers between devices: 76.8 us -> none  [broadcast(): lax.all_gather(shard, axis)]
    all_to_all x1 -> x0, waiting for transfers between devices: 56.5 us -> none  [from_everyone(): return lax.all_to_all(copies, axis, split_axis=0, concat_axis=0, tiled=True)]
    another operation x10 -> x0, other arithmetic: 46 us -> none  [the longest x6 24.9 us: reduce_panel(): factor = jnp.linalg.cholesky(gram)]
    dot_general x14 -> x0, matrix products: 43.1 us -> none  [contract(): lax.dot_general(left, right, (((left_dim,), (right_dim,)), ((), ())), pre...]
    all_to_all x1 -> x0, starting transfers between devices: 9.39 us -> none  [from_everyone(): return lax.all_to_all(copies, axis, split_axis=0, concat_axis=0, tiled=True)]
  transfers between devices with their start and end apart: 9 -> 0, of which waited for: 7 -> 0; matrix products, arithmetic and copies ran while one was open for 12% -> 0% of each run, Pallas kernels for 0% -> 0%
where the time goes in v1:
time: 167 us
  Pallas kernels  161 us (96%)
  local copies, waits for them, and re-layouts  5.59 us (3%)
    pallas_call x1, Pallas kernels, factors_kernel(): pl.pallas_call(kernel, out_shape=(jax.ShapeDtypeStruct((rows, 4 * NB), F3...  152 us
    pallas_call x1, Pallas kernels, update(): pl.pallas_call(update_kernel, grid=(rows // tile,), out_shape=jax.ShapeDt...  8.96 us
    unnamed x6, local copies, waits for them, and re-layouts  5.59 us

profile of v1, /device:TPU:1, one launch (start us, length us, event | category | flops | bytes accessed | tf_op | source)
XLA Modules:
  0.0 166.9 jit_solution(11577685136144943252)
XLA Ops:
  0.0 152.3 %reflector_factors.1 = (f32[512,512]{1,0:T(8,128)}, f32[512,2048]{1,0:T(8,128)}) custom-call(f32[512,2048]{1,0:T(8,128)} %h_ref.1), custom_call_target="tpu_custom_call" | custom-call | tf_op jit(solution)/shard_map/reflector_factors/pallas_call | solution.py:384
  152.3 0.0 copy-start
  152.3 2.2 %copy-done = f32[512,2048]{1,0:T(8,128)S(1)} copy-done((f32[512,2048]{1,0:T(8,128)S(1)}, f32[512,2048]{1,0:T(8,128)}, u32[]{:S(2)}) %copy-start) | copy-done | bytes 4194328
  154.5 0.0 copy-start.1
  154.5 2.2 %copy-done.1 = f32[512,2048]{1,0:T(8,128)S(1)} copy-done((f32[512,2048]{1,0:T(8,128)S(1)}, f32[512,2048]{1,0:T(8,128)}, u32[]{:S(2)}) %copy-start.1) | copy-done | bytes 4194328
  156.7 0.0 copy-start.2
  156.7 1.2 copy-done.2
  157.9 9.0 %apply_factors.1 = f32[512,2048]{1,0:T(8,128)} custom-call(f32[512,2048]{1,0:T(8,128)S(1)} %copy-done, f32[512,512]{1,0:T(8,128)S(1)} %copy-done.2, f32[512,2048]{1,0:T(8,128)S(1)} %copy-done.1), custom_call_target="tpu_custom_call" | custom-call | tf_op jit(solution)/shard_map/apply_factors/pallas_call | solution.py:428
Async XLA Ops:
  152.3 2.2 %copy-start = (f32[512,2048]{1,0:T(8,128)S(1)}, f32[512,2048]{1,0:T(8,128)}, u32[]{:S(2)}) copy-start(f32[512,2048]{1,0:T(8,128)} %h_ref.1) | copy-start | bytes 12582916
  154.5 2.2 %copy-start.1 = (f32[512,2048]{1,0:T(8,128)S(1)}, f32[512,2048]{1,0:T(8,128)}, u32[]{:S(2)}) copy-start(f32[512,2048]{1,0:T(8,128)} %get-tuple-element.8.rhs_ref) | copy-start | bytes 12582916
  156.7 1.2 copy-start.2

commit v2 on v1

v2 whole, which is shorter than its diff:
```python
import functools

import jax
import jax.numpy as jnp
from jax import lax
from jax.experimental import pallas as pl
from jax.experimental.pallas import tpu as pltpu
from jax.sharding import PartitionSpec as P

NB = 128
Z, X, C = 8, 4, 8
SH = 64
MESH = pl.DeviceIdType.MESH
HIGH = lax.Precision.HIGHEST
F32 = jnp.float32


def dot(a, b):
    return lax.dot_general(a, b, (((1,), (0,)), ((), ())), precision=HIGH, preferred_element_type=F32)


def dot_nt(a, b):
    return lax.dot_general(a, b, (((1,), (1,)), ((), ())), precision=HIGH, preferred_element_type=F32)


def dot_tn(a, b):
    return lax.dot_general(a, b, (((0,), (0,)), ((), ())), precision=HIGH, preferred_element_type=F32)


def sweep_steps(a, groups):
    lane = lax.broadcasted_iota(jnp.int32, (NB, NB), 1)
    sub = lax.broadcasted_iota(jnp.int32, (NB, NB), 0)
    lane_row = lax.broadcasted_iota(jnp.int32, (1, NB), 1)

    def group(_, a):
        for t in range(8):
            pivot = 1.0 / a[t : t + 1, t : t + 1]
            row = a[t : t + 1, :] * pivot
            row = jnp.where(lane_row == t, pivot, row)
            column = jnp.broadcast_to(a[:, t : t + 1], (NB, NB))
            column = jnp.where(sub == t, -1.0, column)
            a = jnp.where((lane == t) | (sub == t), 0.0, a) - column * row
        a = pltpu.roll(a, NB - 8, 0)
        return pltpu.roll(a, NB - 8, 1)

    return lax.fori_loop(0, groups, group, a)


def kernel(
    h_hbm, hv, lhs_ref, up,
    sh, yp, cform, ypr, cr, ur, p2r, ab1, part, rsb, ysh, abt, ab,
    pstack, xb, zb, gsum, inv, sc1, sc2,
    h_sem, loc_sem, sc_send, sc_recv, ra_send, ra_recv, sp_send, sp_recv,
    rp_send, rp_recv, rs_send, rs_recv, px_send, px_recv, pz_send, pz_recv, pc_send, pc_recv,
):
    r = lax.axis_index("row")
    c = lax.axis_index("col")
    z = r // X
    x = lax.rem(r, X)
    plane = lax.rem(r, C)
    rel = lax.rem(c - plane + C, C)
    z_up = lax.rem(z + 1, Z)
    z_down = lax.rem(z + Z - 1, Z)
    z_to = jnp.where(rel < 4, z_up, z)
    half = c // 4
    same = lax.rem(z, 2) == half
    z_from = jnp.where(same, z, z_down)

    def remote(src, dst, send, recv, row, col):
        return pltpu.make_async_remote_copy(
            src_ref=src, dst_ref=dst, send_sem=send, recv_sem=recv,
            device_id=(row, col), device_id_type=MESH,
        )

    def landed(ref, send, recv):
        remote(ref, ref, send, recv, r, c).wait_recv()

    def other(d):
        return lax.rem(c + d, C)

    started = []

    def go(copy):
        copy.start()
        started.append(copy)

    copy_h = pltpu.make_async_copy(h_hbm, hv, h_sem)
    copy_h.start()

    barrier = pltpu.get_barrier_semaphore()

    def greet(row, col):
        pl.semaphore_signal(barrier, inc=1, device_id=(row, col), device_id_type=MESH)

    for d in range(1, C):
        greet(r, other(d))
    for i in range(4):
        greet(z_to * X + i, plane)
        greet(z_from * X + lax.rem(c, X), lax.rem(c + jnp.where(same, 4, 0) + i, C))
    for d in range(1, X):
        greet(z * X + lax.rem(x + d, X), c)
    for d in range(1, Z):
        greet(lax.rem(z + d, Z) * X + x, c)
    pl.semaphore_wait(barrier, 25)

    PV, CV, YV, UV = 0, 1, 2, 3

    def column(v, rows):
        if v == CV:
            return cform.at[rows]
        if v == PV:
            return yp.at[rows, NB : 2 * NB]
        return (up if v == UV else yp).at[rows, 0:NB]

    def row(v, rows):
        if v == PV:
            return ypr.at[rows, NB : 2 * NB]
        if v == YV:
            return ypr.at[rows, 0:NB]
        return (cr if v == CV else ur).at[rows]

    def at(start, size):
        return pl.ds(pl.multiple_of(start, 8), size)

    def scatter(v):
        def from_root(d):
            return remote(h_hbm.at[at(SH * other(d), SH), 0:NB], sh.at[v], sc_send.at[v, d], sc_recv.at[v], r, other(d))

        def own():
            return pltpu.make_async_copy(h_hbm.at[at(SH * c, SH), 0:NB], sh.at[v], loc_sem.at[v])

        @pl.when(c == v)
        def _():
            own().start()
            for d in range(1, C):
                from_root(d).start()

        def finish():
            @pl.when(c == v)
            def _():
                own().wait()
                for d in range(1, C):
                    from_root(d).wait_send()

            @pl.when(c != v)
            def _():
                from_root(1).wait_recv()

        return finish

    my_off = ((c // 2) * 4 + r // C) * NB + lax.rem(c, 2) * SH

    def distribute(v, shard):
        for i in range(X):
            to = lax.rem(x + i, X)
            go(remote(
                shard, column(v, at(my_off, SH)),
                sp_send.at[v, i], sp_recv.at[v, lax.rem(rel, 4)], z_to * X + to, plane,
            ))
        mine = row(v, at(SH * c, SH))
        for d in range(1, C):
            go(remote(shard, mine, ra_send.at[v, d], ra_recv.at[v, c], r, other(d)))
        mine[...] = shard[...]

    def wait_rows(v):
        for d in range(1, C):
            landed(row(v, at(SH * other(d), SH)), ra_send.at[v, d], ra_recv.at[v, other(d)])

    def piece(v, block, i):
        aligned = lax.rem(block, 2) == half
        source = jnp.where(aligned, block, lax.rem(block + Z - 1, Z))
        sender = lax.rem(c + jnp.where(aligned, 4, 0) + i, C)
        return column(v, at(((sender // 2) * 4 + source // 2) * NB + lax.rem(sender, 2) * SH, SH))

    def pieces(s, up_way):
        if s < 4:
            return range(4)
        return range(0, 2) if up_way else range(2, 4)

    def ring_copy(v, s, i, up_way, block):
        k = 0 if up_way else 1
        to = z_up if up_way else z_down
        ref = piece(v, block, i)
        return remote(ref, ref, rp_send.at[v, k, s - 1, i], rp_recv.at[v, k, s - 1, i], to * X + x, c)

    def ring_wait_piece(v, s, i, up_way):
        if s == 0:
            landed(piece(v, z, i), sp_send.at[v, 0], sp_recv.at[v, i])
            return
        block = lax.rem(z - s + Z, Z) if up_way else lax.rem(z + s, Z)
        ring_copy(v, s, i, up_way, block).wait_recv()

    def ring(v, s):
        for i in range(4):
            if s == 1:
                ring_wait_piece(v, 0, i, True)
            for up_way in (True, False):
                if i not in pieces(s, up_way):
                    continue
                if s > 1:
                    ring_wait_piece(v, s - 1, i, up_way)
                block = lax.rem(z - (s - 1) + Z, Z) if up_way else lax.rem(z + s - 1, Z)
                go(ring_copy(v, s, i, up_way, block))

    def ring_end(v):
        for up_way in (True, False):
            for i in range(4):
                if i not in pieces(4, up_way):
                    ring_wait_piece(v, 3, i, up_way)
            for i in pieces(4, up_way):
                ring_wait_piece(v, 4, i, up_way)

    def reduce_start(q):
        for d in range(1, C):
            go(remote(part.at[q, at(SH * other(d), SH)], rsb.at[q, d - 1], rs_send.at[q, d], rs_recv.at[q, d], r, other(d)))

    def reduce_end(q):
        total = part[q, at(SH * c, SH), :]
        for d in range(1, C):
            landed(rsb.at[q, d - 1], rs_send.at[q, d], rs_recv.at[q, d])
            total = total + rsb[q, d - 1]
        ysh[q] = total

    sizes = (3 * NB, NB, 3 * NB, NB)

    def sum_start(e):
        m = sizes[e] // C
        xb[e, x, 0:m, :] = pstack[e, at(m * c, m), :]
        for d in range(1, X):
            go(remote(
                pstack.at[e, at(m * c, m)], xb.at[e, x, 0:m], px_send.at[e, d], px_recv.at[e, x],
                z * X + lax.rem(x + d, X), c,
            ))

    def sum_z(e):
        m = sizes[e] // C
        for d in range(1, X):
            k = lax.rem(x + d, X)
            landed(xb.at[e, k, 0:m], px_send.at[e, d], px_recv.at[e, k])
        zb[e, z, 0:m, :] = (xb[e, 0, 0:m, :] + xb[e, 1, 0:m, :]) + (xb[e, 2, 0:m, :] + xb[e, 3, 0:m, :])
        for d in range(1, Z):
            ref = zb.at[e, z, 0:m]
            go(remote(ref, ref, pz_send.at[e, d], pz_recv.at[e, z], lax.rem(z + d, Z) * X + x, c))

    def sum_col(e):
        m = sizes[e] // C
        for d in range(1, Z):
            k = lax.rem(z + d, Z)
            landed(zb.at[e, k, 0:m], pz_send.at[e, d], pz_recv.at[e, k])
        total = zb[e, 0, 0:m, :]
        for k in range(1, Z):
            total = total + zb[e, k, 0:m, :]
        gsum[e, at(m * c, m), :] = total
        for d in range(1, C):
            ref = gsum.at[e, at(m * c, m)]
            go(remote(ref, ref, pc_send.at[e, d], pc_recv.at[e, c], r, other(d)))

    def sum_end(e):
        m = sizes[e] // C
        for d in range(1, C):
            landed(gsum.at[e, at(m * other(d), m)], pc_send.at[e, d], pc_recv.at[e, other(d)])

    def times_h(q, src, first, last):
        @pl.loop(first, last)
        def _(j):
            rows = pl.ds(pl.multiple_of(j * NB, NB), NB)
            part[q, rows, :] = dot(hv[rows, :], src[...])

    eye = lax.broadcasted_iota(jnp.int32, (NB, NB), 0) == lax.broadcasted_iota(jnp.int32, (NB, NB), 1)

    def scaled(q, e):
        gram = gsum[e, 0:NB, :]
        diagonal = jnp.where(eye, gram, 0.0)
        sc1[q] = jnp.broadcast_to(lax.rsqrt(jnp.sum(diagonal, axis=0, keepdims=True)), (NB, NB))
        sc2[q] = jnp.broadcast_to(lax.rsqrt(jnp.sum(diagonal, axis=1, keepdims=True)), (NB, NB))
        inv[q] = gram * sc1[q] * sc2[q]

    def sweep(q, groups):
        inv[q] = sweep_steps(inv[q], groups)

    def factors(p, y, k, s, d):
        pk = dot(p * d[0:1, :], k)
        alpha = -2.0 * pk * d[0:1, :]
        beta = dot(4.0 * dot(pk, s) - 2.0 * (y * d[0:1, :]), k) * d[0:1, :]
        return alpha, beta

    finish_p = scatter(PV)
    finish_c = scatter(CV)
    finish_p()

    @pl.when((r == 0) & (c < 2))
    def _():
        sh[PV] = jnp.zeros((SH, NB), F32)

    distribute(PV, sh.at[PV])
    finish_c()
    distribute(CV, sh.at[CV])
    ring(PV, 1)
    wait_rows(PV)
    wait_rows(CV)
    p1 = ypr[:, NB : 2 * NB]
    pstack[0, 0:NB, :] = dot_tn(p1, p1)
    pstack[0, NB : 2 * NB, :] = dot_tn(cr[...], p1)
    pstack[0, 2 * NB : 3 * NB, :] = jnp.where(r == 1, ypr[0:NB, NB : 2 * NB], 0.0)
    sum_start(0)
    ring(PV, 2)
    sum_z(0)
    ring(PV, 3)
    ring(PV, 4)
    sum_col(0)
    ring_end(PV)
    ring(CV, 1)
    copy_h.wait()
    times_h(0, column(PV, slice(None)), 0, 2)
    ring(CV, 2)
    times_h(0, column(PV, slice(None)), 2, 4)
    reduce_start(0)
    sum_end(0)
    scaled(0, 0)
    sweep(0, 3)
    ring(CV, 3)
    sweep(0, 2)
    reduce_end(0)
    distribute(YV, ysh.at[0])
    ring(CV, 4)
    sweep(0, 4)
    ring(YV, 1)
    wait_rows(YV)
    pstack[1, 0:NB, :] = dot_tn(ypr[:, NB : 2 * NB], ypr[:, 0:NB])
    sum_start(1)
    sweep(0, 3)
    ring(YV, 2)
    sum_z(1)
    sweep(0, 4)
    ring(YV, 3)
    sum_col(1)
    ring(YV, 4)
    sum_end(1)
    k1, d1, e1 = inv[0], sc1[0], sc2[0]
    s1 = gsum[1, 0:NB, :] * d1 * e1
    alpha_b, beta_b = factors(gsum[0, 2 * NB : 3 * NB, :], gsum[0, NB : 2 * NB, :], k1, s1, d1)
    abt[0:NB, :] = alpha_b.T
    abt[NB : 2 * NB, :] = beta_b.T
    p2r[...] = cr[...] + dot(ypr[...], abt[...])

    @pl.when(r < 2)
    def _():
        p2r[0:NB, :] = jnp.zeros((NB, NB), F32)

    pstack[2, 0:NB, :] = dot_tn(p2r[...], p2r[...])
    pstack[2, NB : 3 * NB, :] = dot_tn(ypr[...], p2r[...])
    sum_start(2)
    ring_end(CV)
    ring_end(YV)

    @pl.loop(0, 16)
    def _(k):
        rows = pl.ds(pl.multiple_of(k * NB, NB), NB)
        value = cform[rows, :] + dot(yp[rows, :], abt[...])
        up[rows, NB : 2 * NB] = jnp.where((k == 0) & (c < 2), 0.0, value)

    sum_z(2)
    times_h(1, up.at[:, NB : 2 * NB], 0, 4)
    reduce_start(1)
    sum_col(2)
    alpha1, beta1 = factors(ypr[:, NB : 2 * NB], ypr[:, 0:NB], k1, s1, d1)
    ab1[:, 0:NB] = alpha1
    ab1[:, NB : 2 * NB] = beta1
    reduce_end(1)
    distribute(UV, ysh.at[1])
    sum_end(2)
    scaled(1, 2)
    sweep(1, 4)
    ring(UV, 1)
    wait_rows(UV)
    pstack[3, 0:NB, :] = dot_tn(p2r[...], ur[...])
    sum_start(3)
    sweep(1, 3)
    ring(UV, 2)
    sum_z(3)
    sweep(1, 4)
    ring(UV, 3)
    sum_col(3)
    sweep(1, 5)
    ring(UV, 4)
    k2, d2, e2 = inv[1], sc1[1], sc2[1]
    t1, t2 = gsum[2, NB : 2 * NB, :], gsum[2, 2 * NB : 3 * NB, :]
    kt2 = dot(k1, t2 * e1)
    ab[0:NB, :] = -2.0 * kt2 * e1
    ab[NB : 2 * NB, :] = dot(k1, 4.0 * dot(s1, kt2) - 2.0 * (t1 * e1)) * e1
    pk2 = dot(p2r[...] * d2[0:1, :], k2)
    alpha2 = -2.0 * pk2 * d2[0:1, :]
    lhs_ref[:, 0:NB] = alpha2
    ab1[...] = ab1[...] + dot_nt(alpha2, ab[...])
    y2 = ur[...] + dot(ypr[...], ab[...])

    @pl.loop(0, 8)
    def _(k):
        cols = pl.ds(pl.multiple_of(k * 2 * NB, 2 * NB), 2 * NB)
        hv[:, cols] = hv[:, cols] + dot_nt(ab1[...], yp[cols, :])

    sum_end(3)
    s2 = (gsum[3, 0:NB, :] + dot_tn(gsum[2, NB : 3 * NB, :], ab[...])) * d2 * e2
    lhs_ref[:, NB : 2 * NB] = dot(4.0 * dot(pk2, s2) - 2.0 * (y2 * d2[0:1, :]), k2) * d2[0:1, :]
    ring_end(UV)
    for copy in started:
        copy.wait_send()


def factors_kernel(hamiltonian):
    rows, cols = hamiltonian.shape
    dma = pltpu.SemaphoreType.DMA
    vmem = pl.BlockSpec(memory_space=pltpu.VMEM)
    return pl.pallas_call(
        kernel,
        out_shape=(
            pltpu.VMEM((rows, cols), F32),
            pltpu.VMEM((rows, 2 * NB), F32),
            pltpu.VMEM((cols, 2 * NB), F32),
        ),
        in_specs=[pl.BlockSpec(memory_space=pltpu.HBM)],
        out_specs=(vmem, vmem, vmem),
        scratch_shapes=[
            pltpu.VMEM((2, SH, NB), F32),
            pltpu.VMEM((cols, 2 * NB), F32),
            pltpu.VMEM((cols, NB), F32),
            pltpu.VMEM((rows, 2 * NB), F32),
            pltpu.VMEM((rows, NB), F32),
            pltpu.VMEM((rows, NB), F32),
            pltpu.VMEM((rows, NB), F32),
            pltpu.VMEM((rows, 2 * NB), F32),
            pltpu.VMEM((2, rows, NB), F32),
            pltpu.VMEM((2, C - 1, SH, NB), F32),
            pltpu.VMEM((2, SH, NB), F32),
            pltpu.VMEM((2 * NB, NB), F32),
            pltpu.VMEM((2 * NB, NB), F32),
            pltpu.VMEM((4, 3 * NB, NB), F32),
            pltpu.VMEM((4, X, 3 * NB // C, NB), F32),
            pltpu.VMEM((4, Z, 3 * NB // C, NB), F32),
            pltpu.VMEM((4, 3 * NB, NB), F32),
            pltpu.VMEM((2, NB, NB), F32),
            pltpu.VMEM((2, NB, NB), F32),
            pltpu.VMEM((2, NB, NB), F32),
            dma, dma((2,)), dma((2, C)), dma((2,)),
            dma((4, C)), dma((4, C)), dma((4, 4)), dma((4, 4)),
            dma((4, 2, 4, 4)), dma((4, 2, 4, 4)),
            dma((2, C)), dma((2, C)),
            dma((4, X)), dma((4, X)), dma((4, Z)), dma((4, Z)), dma((4, C)), dma((4, C)),
        ],
        compiler_params=pltpu.CompilerParams(
            collective_id=0, has_side_effects=True, vmem_limit_bytes=32 * 1024 * 1024
        ),
        name="reflector_factors",
    )(hamiltonian)


def update_kernel(h_ref, lhs_ref, up_ref, out_ref):
    cols = pl.ds(pl.multiple_of(pl.program_id(0) * 2 * NB, 2 * NB), 2 * NB)
    out_ref[...] = h_ref[:, cols] + dot_nt(lhs_ref[...], up_ref[cols, :])


def update(partly, lhs, up):
    rows, cols = partly.shape
    vmem = pl.BlockSpec(memory_space=pltpu.VMEM)
    return pl.pallas_call(
        update_kernel,
        grid=(cols // (2 * NB),),
        out_shape=jax.ShapeDtypeStruct((rows, cols), F32),
        in_specs=[vmem, vmem, vmem],
        out_specs=pl.BlockSpec((rows, 2 * NB), lambda i: (0, i)),
        compiler_params=pltpu.CompilerParams(vmem_limit_bytes=24 * 1024 * 1024),
        name="apply_factors",
    )(partly, lhs, up)


def body(hamiltonian):
    return update(*factors_kernel(pltpu.with_memory_space_constraint(hamiltonian, pltpu.HBM)))


def solution(mesh):
    return jax.shard_map(
        body, mesh=mesh, in_specs=(P("row", "col"),), out_specs=P("row", "col"), check_vma=False
    )
```

time: 167 us -> 138 us (0.83)
  Pallas kernels: 161 us -> 138 us
  local copies, waits for them, and re-layouts: 5.59 us -> 0 us
    pallas_call x2, Pallas kernels: 161 us -> 138 us  [the longest x1 131 us: factors_kernel(): pl.pallas_call(kernel, out_shape=(pltpu.VMEM((rows, cols), F32), pltpu.VM...]
    unnamed x6 -> x0, local copies, waits for them, and re-layouts: 5.59 us -> none
where the time goes in v2:
time: 138 us
  Pallas kernels  138 us (100%)
    pallas_call x1, Pallas kernels, factors_kernel(): pl.pallas_call(kernel, out_shape=(pltpu.VMEM((rows, cols), F32), pltpu.VM...  131 us
    pallas_call x1, Pallas kernels, update(): pl.pallas_call(update_kernel, grid=(cols // (2 * NB),), out_shape=jax.Sha...  6.32 us

profile of v2, /device:TPU:1, one launch (start us, length us, event | category | flops | bytes accessed | tf_op | source)
XLA Modules:
  0.0 137.5 jit_solution(14728483823122017667)
XLA Ops:
  0.0 131.2 %reflector_factors.1 = (f32[512,2048]{1,0:T(8,128)S(1)}, f32[512,256]{1,0:T(8,128)S(1)}, f32[2048,256]{1,0:T(8,128)S(1)}) custom-call(f32[512,2048]{1,0:T(8,128)} %h_hbm.1), custom_call_target="tpu_custom_call" | custom-call | tf_op jit(solution)/shard_map/reflector_factors/pallas_call | solution.py:414
  131.2 6.3 %apply_factors.1 = f32[512,2048]{1,0:T(8,128)} custom-call(f32[512,2048]{1,0:T(8,128)S(1)} %get-tuple-element.8.h_ref, f32[512,256]{1,0:T(8,128)S(1)} %get-tuple-element.9.lhs_ref, f32[2048,256]{1,0:T(8,128)S(1)} %get-tuple-element.10.up_ref), custom_call_target="tpu_custom_call" | custom-call | tf_op jit(solution)/shard_map/apply_factors/pallas_call | solution.py:465

commit v3 on v2

--- a/solution.py
+++ b/solution.py
@@ -13,6 +13,7 @@
 MESH = pl.DeviceIdType.MESH
 HIGH = lax.Precision.HIGHEST
 F32 = jnp.float32
+BF16 = jnp.bfloat16
 
 
 def dot(a, b):
@@ -27,29 +28,47 @@
     return lax.dot_general(a, b, (((0,), (0,)), ((), ())), precision=HIGH, preferred_element_type=F32)
 
 
+def dot_b(a, b, contract):
+    return lax.dot_general(a, b, (contract, ((), ())), preferred_element_type=F32)
+
+
+def halves(value):
+    high = value.astype(BF16)
+    return high, (value - high.astype(F32)).astype(BF16)
+
+
 def sweep_steps(a, groups):
-    lane = lax.broadcasted_iota(jnp.int32, (NB, NB), 1)
-    sub = lax.broadcasted_iota(jnp.int32, (NB, NB), 0)
-    lane_row = lax.broadcasted_iota(jnp.int32, (1, NB), 1)
+    tile = (8, NB)
+    lane = lax.broadcasted_iota(jnp.int32, tile, 1)
+    sub = lax.broadcasted_iota(jnp.int32, tile, 0)
 
     def group(_, a):
-        for t in range(8):
-            pivot = 1.0 / a[t : t + 1, t : t + 1]
-            row = a[t : t + 1, :] * pivot
-            row = jnp.where(lane_row == t, pivot, row)
-            column = jnp.broadcast_to(a[:, t : t + 1], (NB, NB))
-            column = jnp.where(sub == t, -1.0, column)
-            a = jnp.where((lane == t) | (sub == t), 0.0, a) - column * row
-        a = pltpu.roll(a, NB - 8, 0)
-        return pltpu.roll(a, NB - 8, 1)
-
-    return lax.fori_loop(0, groups, group, a)
+        for t in range(0, 8, 2):
+            r0 = jnp.broadcast_to(a[0, t : t + 1, :], tile)
+            r1 = jnp.broadcast_to(a[0, t + 1 : t + 2, :], tile)
+            p = jnp.broadcast_to(r0[:, t : t + 1], tile)
+            q = jnp.broadcast_to(r0[:, t + 1 : t + 2], tile)
+            s = jnp.broadcast_to(r1[:, t + 1 : t + 2], tile)
+            scale = 1.0 / (p * s - q * q)
+            i00, i01, i11 = s * scale, -q * scale, p * scale
+            n0 = jnp.where(lane == t, i00, jnp.where(lane == t + 1, i01, i00 * r0 + i01 * r1))
+            n1 = jnp.where(lane == t, i01, jnp.where(lane == t + 1, i11, i01 * r0 + i11 * r1))
+            c0 = jnp.broadcast_to(a[:, :, t : t + 1], a.shape)
+            c1 = jnp.broadcast_to(a[:, :, t + 1 : t + 2], a.shape)
+            pivot_lane = ((lane == t) | (lane == t + 1))[None]
+            rest = jnp.where(pivot_lane, 0.0, a) - c0 * n0[None] - c1 * n1[None]
+            top = jnp.where(sub == t, n0, jnp.where(sub == t + 1, n1, rest[0]))
+            a = jnp.concatenate([top[None], rest[1:]], axis=0)
+        a = jnp.concatenate([a[1:], a[:1]], axis=0)
+        return pltpu.roll(a, NB - 8, 2)
+
+    return lax.fori_loop(0, groups, group, a.reshape(NB // 8, 8, NB)).reshape(NB, NB)
 
 
 def kernel(
     h_hbm, hv, lhs_ref, up,
     sh, yp, cform, ypr, cr, ur, p2r, ab1, part, rsb, ysh, abt, ab,
-    pstack, xb, zb, gsum, inv, sc1, sc2,
+    pstack, xb, zb, gsum, inv, sc1, sc2, hh, hl, vs, abts, abh,
     h_sem, loc_sem, sc_send, sc_recv, ra_send, ra_recv, sp_send, sp_recv,
     rp_send, rp_recv, rs_send, rs_recv, px_send, px_recv, pz_send, pz_recv, pc_send, pc_recv,
 ):
@@ -221,7 +240,7 @@
             total = total + rsb[q, d - 1]
         ysh[q] = total
 
-    sizes = (3 * NB, NB, 3 * NB, NB)
+    sizes = (2 * NB, 2 * NB, 3 * NB, NB)
 
     def sum_start(e):
         m = sizes[e] // C
@@ -260,11 +279,23 @@
         for d in range(1, C):
             landed(gsum.at[e, at(m * other(d), m)], pc_send.at[e, d], pc_recv.at[e, other(d)])
 
-    def times_h(q, src, first, last):
-        @pl.loop(first, last)
+    inner = ((1,), (0,))
+    both_last = ((1,), (1,))
+
+    def fold(value):
+        return value[:, 0:NB] + value[:, NB : 2 * NB]
+
+    def split_h():
+        @pl.loop(0, 8)
         def _(j):
-            rows = pl.ds(pl.multiple_of(j * NB, NB), NB)
-            part[q, rows, :] = dot(hv[rows, :], src[...])
+            rows = pl.ds(pl.multiple_of(j * SH, SH), SH)
+            hh[rows, :], hl[rows, :] = halves(hv[rows, :])
+
+    def times_h(q):
+        @pl.loop(0, 2)
+        def _(j):
+            rows = pl.ds(pl.multiple_of(j * 2 * NB, 2 * NB), 2 * NB)
+            part[q, rows, :] = fold(dot_b(hh[rows, :], vs[...], inner) + dot_b(hl[rows, :], vs[...], inner))
 
     eye = lax.broadcasted_iota(jnp.int32, (NB, NB), 0) == lax.broadcasted_iota(jnp.int32, (NB, NB), 1)
 
@@ -293,54 +324,59 @@
         sh[PV] = jnp.zeros((SH, NB), F32)
 
     distribute(PV, sh.at[PV])
-    finish_c()
-    distribute(CV, sh.at[CV])
     ring(PV, 1)
     wait_rows(PV)
-    wait_rows(CV)
     p1 = ypr[:, NB : 2 * NB]
     pstack[0, 0:NB, :] = dot_tn(p1, p1)
-    pstack[0, NB : 2 * NB, :] = dot_tn(cr[...], p1)
-    pstack[0, 2 * NB : 3 * NB, :] = jnp.where(r == 1, ypr[0:NB, NB : 2 * NB], 0.0)
+    pstack[0, NB : 2 * NB, :] = jnp.where(r == 1, ypr[0:NB, NB : 2 * NB], 0.0)
     sum_start(0)
     ring(PV, 2)
     sum_z(0)
     ring(PV, 3)
+    finish_c()
+    distribute(CV, sh.at[CV])
+    copy_h.wait()
+    split_h()
     ring(PV, 4)
     sum_col(0)
     ring_end(PV)
-    ring(CV, 1)
-    copy_h.wait()
-    times_h(0, column(PV, slice(None)), 0, 2)
-    ring(CV, 2)
-    times_h(0, column(PV, slice(None)), 2, 4)
+
+    @pl.loop(0, 8)
+    def _(k):
+        rows = pl.ds(pl.multiple_of(k * 2 * NB, 2 * NB), 2 * NB)
+        vs[rows, 0:NB], vs[rows, NB : 2 * NB] = halves(yp[rows, NB : 2 * NB])
+
+    times_h(0)
     reduce_start(0)
     sum_end(0)
     scaled(0, 0)
-    sweep(0, 3)
-    ring(CV, 3)
-    sweep(0, 2)
+    ring(CV, 1)
+    sweep(0, 4)
     reduce_end(0)
     distribute(YV, ysh.at[0])
-    ring(CV, 4)
-    sweep(0, 4)
+    ring(CV, 2)
+    sweep(0, 6)
     ring(YV, 1)
+    ring(CV, 3)
+    wait_rows(CV)
     wait_rows(YV)
     pstack[1, 0:NB, :] = dot_tn(ypr[:, NB : 2 * NB], ypr[:, 0:NB])
+    pstack[1, NB : 2 * NB, :] = dot_tn(cr[...], ypr[:, NB : 2 * NB])
     sum_start(1)
-    sweep(0, 3)
+    sweep(0, 6)
     ring(YV, 2)
+    ring(CV, 4)
     sum_z(1)
-    sweep(0, 4)
     ring(YV, 3)
     sum_col(1)
     ring(YV, 4)
     sum_end(1)
     k1, d1, e1 = inv[0], sc1[0], sc2[0]
     s1 = gsum[1, 0:NB, :] * d1 * e1
-    alpha_b, beta_b = factors(gsum[0, 2 * NB : 3 * NB, :], gsum[0, NB : 2 * NB, :], k1, s1, d1)
+    alpha_b, beta_b = factors(gsum[0, NB : 2 * NB, :], gsum[1, NB : 2 * NB, :], k1, s1, d1)
     abt[0:NB, :] = alpha_b.T
     abt[NB : 2 * NB, :] = beta_b.T
+    abts[:, 0:NB], abts[:, NB : 2 * NB] = halves(abt[...])
     p2r[...] = cr[...] + dot(ypr[...], abt[...])
 
     @pl.when(r < 2)
@@ -353,14 +389,18 @@
     ring_end(CV)
     ring_end(YV)
 
-    @pl.loop(0, 16)
+    @pl.loop(0, 8)
     def _(k):
-        rows = pl.ds(pl.multiple_of(k * NB, NB), NB)
-        value = cform[rows, :] + dot(yp[rows, :], abt[...])
-        up[rows, NB : 2 * NB] = jnp.where((k == 0) & (c < 2), 0.0, value)
+        rows = pl.ds(pl.multiple_of(k * 2 * NB, 2 * NB), 2 * NB)
+        high, low = halves(yp[rows, :])
+        value = cform[rows, :] + fold(dot_b(high, abts[...], inner) + dot_b(low, abts[...], inner))
+        sub = lax.broadcasted_iota(jnp.int32, (2 * NB, NB), 0)
+        value = jnp.where((sub < NB) & (k == 0) & (c < 2), 0.0, value)
+        up[rows, NB : 2 * NB] = value
+        vs[rows, 0:NB], vs[rows, NB : 2 * NB] = halves(value)
 
     sum_z(2)
-    times_h(1, up.at[:, NB : 2 * NB], 0, 4)
+    times_h(1)
     reduce_start(1)
     sum_col(2)
     alpha1, beta1 = factors(ypr[:, NB : 2 * NB], ypr[:, 0:NB], k1, s1, d1)
@@ -375,14 +415,12 @@
     wait_rows(UV)
     pstack[3, 0:NB, :] = dot_tn(p2r[...], ur[...])
     sum_start(3)
-    sweep(1, 3)
+    sweep(1, 6)
     ring(UV, 2)
     sum_z(3)
-    sweep(1, 4)
+    sweep(1, 6)
     ring(UV, 3)
     sum_col(3)
-    sweep(1, 5)
-    ring(UV, 4)
     k2, d2, e2 = inv[1], sc1[1], sc2[1]
     t1, t2 = gsum[2, NB : 2 * NB, :], gsum[2, 2 * NB : 3 * NB, :]
     kt2 = dot(k1, t2 * e1)
@@ -390,18 +428,23 @@
     ab[NB : 2 * NB, :] = dot(k1, 4.0 * dot(s1, kt2) - 2.0 * (t1 * e1)) * e1
     pk2 = dot(p2r[...] * d2[0:1, :], k2)
     alpha2 = -2.0 * pk2 * d2[0:1, :]
-    lhs_ref[:, 0:NB] = alpha2
-    ab1[...] = ab1[...] + dot_nt(alpha2, ab[...])
+    lhs_ref[0, :, 0:NB], lhs_ref[1, :, 0:NB] = halves(alpha2)
+    abh[0], abh[1] = halves(ab1[...] + dot_nt(alpha2, ab[...]))
     y2 = ur[...] + dot(ypr[...], ab[...])
+    ring(UV, 4)
 
     @pl.loop(0, 8)
     def _(k):
         cols = pl.ds(pl.multiple_of(k * 2 * NB, 2 * NB), 2 * NB)
-        hv[:, cols] = hv[:, cols] + dot_nt(ab1[...], yp[cols, :])
+        high, low = halves(yp[cols, :])
+        hv[:, cols] = hv[:, cols] + (
+            dot_b(abh[0], high, both_last) + (dot_b(abh[0], low, both_last) + dot_b(abh[1], high, both_last))
+        )
 
     sum_end(3)
     s2 = (gsum[3, 0:NB, :] + dot_tn(gsum[2, NB : 3 * NB, :], ab[...])) * d2 * e2
-    lhs_ref[:, NB : 2 * NB] = dot(4.0 * dot(pk2, s2) - 2.0 * (y2 * d2[0:1, :]), k2) * d2[0:1, :]
+    beta2 = dot(4.0 * dot(pk2, s2) - 2.0 * (y2 * d2[0:1, :]), k2) * d2[0:1, :]
+    lhs_ref[0, :, NB : 2 * NB], lhs_ref[1, :, NB : 2 * NB] = halves(beta2)
     ring_end(UV)
     for copy in started:
         copy.wait_send()
@@ -415,7 +458,7 @@
         kernel,
         out_shape=(
             pltpu.VMEM((rows, cols), F32),
-            pltpu.VMEM((rows, 2 * NB), F32),
+            pltpu.VMEM((2, rows, 2 * NB), BF16),
             pltpu.VMEM((cols, 2 * NB), F32),
         ),
         in_specs=[pl.BlockSpec(memory_space=pltpu.HBM)],
@@ -441,6 +484,11 @@
             pltpu.VMEM((2, NB, NB), F32),
             pltpu.VMEM((2, NB, NB), F32),
             pltpu.VMEM((2, NB, NB), F32),
+            pltpu.VMEM((rows, cols), BF16),
+            pltpu.VMEM((rows, cols), BF16),
+            pltpu.VMEM((cols, 2 * NB), BF16),
+            pltpu.VMEM((2 * NB, 2 * NB), BF16),
+            pltpu.VMEM((2, rows, 2 * NB), BF16),
             dma, dma((2,)), dma((2, C)), dma((2,)),
             dma((4, C)), dma((4, C)), dma((4, 4)), dma((4, 4)),
             dma((4, 2, 4, 4)), dma((4, 2, 4, 4)),
@@ -448,7 +496,7 @@
             dma((4, X)), dma((4, X)), dma((4, Z)), dma((4, Z)), dma((4, C)), dma((4, C)),
         ],
         compiler_params=pltpu.CompilerParams(
-            collective_id=0, has_side_effects=True, vmem_limit_bytes=32 * 1024 * 1024
+            collective_id=0, has_side_effects=True, vmem_limit_bytes=36 * 1024 * 1024
         ),
         name="reflector_factors",
     )(hamiltonian)
@@ -456,7 +504,11 @@
 
 def update_kernel(h_ref, lhs_ref, up_ref, out_ref):
     cols = pl.ds(pl.multiple_of(pl.program_id(0) * 2 * NB, 2 * NB), 2 * NB)
-    out_ref[...] = h_ref[:, cols] + dot_nt(lhs_ref[...], up_ref[cols, :])
+    high, low = halves(up_ref[cols, :])
+    last = ((1,), (1,))
+    out_ref[...] = h_ref[:, cols] + (
+        dot_b(lhs_ref[0], high, last) + (dot_b(lhs_ref[0], low, last) + dot_b(lhs_ref[1], high, last))
+    )
 
 
 def update(partly, lhs, up):
@@ -468,7 +520,7 @@
         out_shape=jax.ShapeDtypeStruct((rows, cols), F32),
         in_specs=[vmem, vmem, vmem],
         out_specs=pl.BlockSpec((rows, 2 * NB), lambda i: (0, i)),
-        compiler_params=pltpu.CompilerParams(vmem_limit_bytes=24 * 1024 * 1024),
+        compiler_params=pltpu.CompilerParams(vmem_limit_bytes=20 * 1024 * 1024),
         name="apply_factors",
     )(partly, lhs, up)
 

time: 138 us -> 126 us (0.913)
  Pallas kernels: 138 us -> 126 us
    pallas_call x1, Pallas kernels: 131 us -> 121 us  [factors_kernel(): pl.pallas_call(kernel, out_shape=(pltpu.VMEM((rows, cols), F32), pltpu.VM...]
where the time goes in v3:
time: 126 us
  Pallas kernels  126 us (100%)
    pallas_call x1, Pallas kernels, factors_kernel(): pl.pallas_call(kernel, out_shape=(pltpu.VMEM((rows, cols), F32), pltpu.VM...  121 us
    pallas_call x1, Pallas kernels, update(): pl.pallas_call(update_kernel, grid=(cols // (2 * NB),), out_shape=jax.Sha...  5.24 us

profile of v3, /device:TPU:1, one launch (start us, length us, event | category | flops | bytes accessed | tf_op | source)
XLA Modules:
  0.0 125.9 jit_solution(13465190435158906844)
XLA Ops:
  0.0 120.6 %reflector_factors.1 = (f32[512,2048]{1,0:T(8,128)S(1)}, bf16[2,512,256]{2,1,0:T(8,128)(2,1)S(1)}, f32[2048,256]{1,0:T(8,128)S(1)}) custom-call(f32[512,2048]{1,0:T(8,128)} %h_hbm.1), custom_call_target="tpu_custom_call" | custom-call | tf_op jit(solution)/shard_map/reflector_factors/pallas_call | solution.py:457
  120.6 5.2 %apply_factors.1 = f32[512,2048]{1,0:T(8,128)} custom-call(f32[512,2048]{1,0:T(8,128)S(1)} %get-tuple-element.8.h_ref, bf16[2,512,256]{2,1,0:T(8,128)(2,1)S(1)} %get-tuple-element.9.lhs_ref, f32[2048,256]{1,0:T(8,128)S(1)} %get-tuple-element.10.up_ref), custom_call_target="tpu_custom_call" | custom-call | tf_op jit(solution)/shard_map/apply_factors/pallas_call | solution.py:517

commit v4 on v3

--- a/solution.py
+++ b/solution.py
@@ -10,6 +10,7 @@
 NB = 128
 Z, X, C = 8, 4, 8
 SH = 64
+HS = 32
 MESH = pl.DeviceIdType.MESH
 HIGH = lax.Precision.HIGHEST
 F32 = jnp.float32
@@ -37,27 +38,49 @@
     return high, (value - high.astype(F32)).astype(BF16)
 
 
+def invert4(m):
+    f = 1.0 / (m[0, 0] * m[1, 1] - m[0, 1] * m[0, 1])
+    a00, a01, a11 = m[1, 1] * f, -m[0, 1] * f, m[0, 0] * f
+    t00, t01 = a00 * m[0, 2] + a01 * m[1, 2], a00 * m[0, 3] + a01 * m[1, 3]
+    t10, t11 = a01 * m[0, 2] + a11 * m[1, 2], a01 * m[0, 3] + a11 * m[1, 3]
+    s00 = m[2, 2] - (m[0, 2] * t00 + m[1, 2] * t10)
+    s01 = m[2, 3] - (m[0, 2] * t01 + m[1, 2] * t11)
+    s11 = m[3, 3] - (m[0, 3] * t01 + m[1, 3] * t11)
+    g = 1.0 / (s00 * s11 - s01 * s01)
+    u00, u01, u11 = s11 * g, -s01 * g, s00 * g
+    w00, w01 = -(t00 * u00 + t01 * u01), -(t00 * u01 + t01 * u11)
+    w10, w11 = -(t10 * u00 + t11 * u01), -(t10 * u01 + t11 * u11)
+    x00 = a00 - (w00 * t00 + w01 * t01)
+    x01 = a01 - (w00 * t10 + w01 * t11)
+    x11 = a11 - (w10 * t10 + w11 * t11)
+    return ((x00, x01, w00, w01), (x01, x11, w10, w11), (w00, w10, u00, u01), (w01, w11, u01, u11))
+
+
 def sweep_steps(a, groups):
     tile = (8, NB)
     lane = lax.broadcasted_iota(jnp.int32, tile, 1)
     sub = lax.broadcasted_iota(jnp.int32, tile, 0)
 
     def group(_, a):
-        for t in range(0, 8, 2):
-            r0 = jnp.broadcast_to(a[0, t : t + 1, :], tile)
-            r1 = jnp.broadcast_to(a[0, t + 1 : t + 2, :], tile)
-            p = jnp.broadcast_to(r0[:, t : t + 1], tile)
-            q = jnp.broadcast_to(r0[:, t + 1 : t + 2], tile)
-            s = jnp.broadcast_to(r1[:, t + 1 : t + 2], tile)
-            scale = 1.0 / (p * s - q * q)
-            i00, i01, i11 = s * scale, -q * scale, p * scale
-            n0 = jnp.where(lane == t, i00, jnp.where(lane == t + 1, i01, i00 * r0 + i01 * r1))
-            n1 = jnp.where(lane == t, i01, jnp.where(lane == t + 1, i11, i01 * r0 + i11 * r1))
-            c0 = jnp.broadcast_to(a[:, :, t : t + 1], a.shape)
-            c1 = jnp.broadcast_to(a[:, :, t + 1 : t + 2], a.shape)
-            pivot_lane = ((lane == t) | (lane == t + 1))[None]
-            rest = jnp.where(pivot_lane, 0.0, a) - c0 * n0[None] - c1 * n1[None]
-            top = jnp.where(sub == t, n0, jnp.where(sub == t + 1, n1, rest[0]))
+        for t in (0, 4):
+            rows = [jnp.broadcast_to(a[0, t + i : t + i + 1, :], tile) for i in range(4)]
+            block = {
+                (i, j): jnp.broadcast_to(rows[i][:, t + j : t + j + 1], tile) for i in range(4) for j in range(i, 4)
+            }
+            inverse = invert4(block)
+            pivot_lane = (lane >= t) & (lane < t + 4)
+            rest = jnp.where(pivot_lane[None], 0.0, a)
+            new = []
+            for i in range(4):
+                v = inverse[i]
+                n = (v[0] * rows[0] + v[1] * rows[1]) + (v[2] * rows[2] + v[3] * rows[3])
+                for j in range(4):
+                    n = jnp.where(lane == t + j, v[j], n)
+                new.append(n)
+                rest = rest - jnp.broadcast_to(a[:, :, t + i : t + i + 1], a.shape) * n[None]
+            top = rest[0]
+            for i in range(4):
+                top = jnp.where(sub == t + i, new[i], top)
             a = jnp.concatenate([top[None], rest[1:]], axis=0)
         a = jnp.concatenate([a[1:], a[:1]], axis=0)
         return pltpu.roll(a, NB - 8, 2)
@@ -69,8 +92,8 @@
     h_hbm, hv, lhs_ref, up,
     sh, yp, cform, ypr, cr, ur, p2r, ab1, part, rsb, ysh, abt, ab,
     pstack, xb, zb, gsum, inv, sc1, sc2, hh, hl, vs, abts, abh,
-    h_sem, loc_sem, sc_send, sc_recv, ra_send, ra_recv, sp_send, sp_recv,
-    rp_send, rp_recv, rs_send, rs_recv, px_send, px_recv, pz_send, pz_recv, pc_send, pc_recv,
+    h_sem, loc_sem, sc_send, sc_recv, v_send, ra_recv, sp_recv, rp_recv, rx_recv,
+    rs_send, rs_recv, p_send, px_recv, pz_recv, pc_recv,
 ):
     r = lax.axis_index("row")
     c = lax.axis_index("col")
@@ -91,17 +114,15 @@
             device_id=(row, col), device_id_type=MESH,
         )
 
-    def landed(ref, send, recv):
-        remote(ref, ref, send, recv, r, c).wait_recv()
+    def landed(rows, sem):
+        ref = cform.at[pl.ds(0, rows)]
+        remote(ref, ref, sem, sem, r, c).wait_recv()
 
     def other(d):
         return lax.rem(c + d, C)
 
-    started = []
-
     def go(copy):
         copy.start()
-        started.append(copy)
 
     copy_h = pltpu.make_async_copy(h_hbm, hv, h_sem)
     copy_h.start()
@@ -143,7 +164,7 @@
 
     def scatter(v):
         def from_root(d):
-            return remote(h_hbm.at[at(SH * other(d), SH), 0:NB], sh.at[v], sc_send.at[v, d], sc_recv.at[v], r, other(d))
+            return remote(h_hbm.at[at(SH * other(d), SH), 0:NB], sh.at[v], sc_send.at[v], sc_recv.at[v], r, other(d))
 
         def own():
             return pltpu.make_async_copy(h_hbm.at[at(SH * c, SH), 0:NB], sh.at[v], loc_sem.at[v])
@@ -158,8 +179,8 @@
             @pl.when(c == v)
             def _():
                 own().wait()
-                for d in range(1, C):
-                    from_root(d).wait_send()
+                ref = cform.at[pl.ds(0, (C - 1) * SH)]
+                remote(ref, ref, sc_send.at[v], sc_recv.at[v], r, c).wait_send()
 
             @pl.when(c != v)
             def _():
@@ -172,112 +193,123 @@
     def distribute(v, shard):
         for i in range(X):
             to = lax.rem(x + i, X)
+            part_of = HS * lax.rem(to, 2)
             go(remote(
-                shard, column(v, at(my_off, SH)),
-                sp_send.at[v, i], sp_recv.at[v, lax.rem(rel, 4)], z_to * X + to, plane,
+                shard.at[at(part_of, HS)], column(v, at(my_off + part_of, HS)),
+                v_send.at[v], sp_recv.at[v, lax.rem(rel, 4) // 2], z_to * X + to, plane,
             ))
         mine = row(v, at(SH * c, SH))
         for d in range(1, C):
-            go(remote(shard, mine, ra_send.at[v, d], ra_recv.at[v, c], r, other(d)))
+            go(remote(shard, mine, v_send.at[v], ra_recv.at[v], r, other(d)))
         mine[...] = shard[...]
 
     def wait_rows(v):
-        for d in range(1, C):
-            landed(row(v, at(SH * other(d), SH)), ra_send.at[v, d], ra_recv.at[v, other(d)])
+        landed((C - 1) * SH, ra_recv.at[v])
 
     def piece(v, block, i):
         aligned = lax.rem(block, 2) == half
         source = jnp.where(aligned, block, lax.rem(block + Z - 1, Z))
         sender = lax.rem(c + jnp.where(aligned, 4, 0) + i, C)
-        return column(v, at(((sender // 2) * 4 + source // 2) * NB + lax.rem(sender, 2) * SH, SH))
-
-    def pieces(s, up_way):
-        if s < 4:
-            return range(4)
-        return range(0, 2) if up_way else range(2, 4)
-
-    def ring_copy(v, s, i, up_way, block):
+        off = ((sender // 2) * 4 + source // 2) * NB + lax.rem(sender, 2) * SH + HS * lax.rem(x, 2)
+        return column(v, at(off, HS))
+
+    def pass_z(v, s, i, up_way, block):
         k = 0 if up_way else 1
         to = z_up if up_way else z_down
         ref = piece(v, block, i)
-        return remote(ref, ref, rp_send.at[v, k, s - 1, i], rp_recv.at[v, k, s - 1, i], to * X + x, c)
-
-    def ring_wait_piece(v, s, i, up_way):
-        if s == 0:
-            landed(piece(v, z, i), sp_send.at[v, 0], sp_recv.at[v, i])
-            return
-        block = lax.rem(z - s + Z, Z) if up_way else lax.rem(z + s, Z)
-        ring_copy(v, s, i, up_way, block).wait_recv()
+        go(remote(ref, ref, v_send.at[v], rp_recv.at[v, k, s - 1, i // 2], to * X + x, c))
+
+    def pass_x(v, i, block):
+        to = lax.rem(x + (1 if i < 2 else X - 1), X)
+        ref = piece(v, block, i)
+        go(remote(ref, ref, v_send.at[v], rx_recv.at[v], z * X + to, c))
+
+    def behind(s, up_way):
+        return lax.rem(z - s + Z, Z) if up_way else lax.rem(z + s, Z)
 
     def ring(v, s):
-        for i in range(4):
+        for g in (0, 1):
+            pair = (2 * g, 2 * g + 1)
             if s == 1:
-                ring_wait_piece(v, 0, i, True)
+                landed(2 * HS, sp_recv.at[v, g])
+                for i in pair:
+                    pass_z(v, 1, i, True, z)
+                    pass_z(v, 1, i, False, z)
+                for i in pair:
+                    pass_x(v, i, z)
+                continue
             for up_way in (True, False):
-                if i not in pieces(s, up_way):
-                    continue
-                if s > 1:
-                    ring_wait_piece(v, s - 1, i, up_way)
-                block = lax.rem(z - (s - 1) + Z, Z) if up_way else lax.rem(z + s - 1, Z)
-                go(ring_copy(v, s, i, up_way, block))
-
-    def ring_end(v):
+                landed(2 * HS, rp_recv.at[v, 0 if up_way else 1, s - 2, g])
+                if s < 4 or up_way == (g == 0):
+                    for i in pair:
+                        pass_z(v, s, i, up_way, behind(s - 1, up_way))
+                for i in pair:
+                    pass_x(v, i, behind(s - 1, up_way))
+
+    def ring_last(v):
         for up_way in (True, False):
-            for i in range(4):
-                if i not in pieces(4, up_way):
-                    ring_wait_piece(v, 3, i, up_way)
-            for i in pieces(4, up_way):
-                ring_wait_piece(v, 4, i, up_way)
+            g = 0 if up_way else 1
+            landed(2 * HS, rp_recv.at[v, g, 3, g])
+            for i in (2 * g, 2 * g + 1):
+                pass_x(v, i, behind(4, up_way))
+
+    def ring_done(v):
+        landed(32 * HS, rx_recv.at[v])
 
     def reduce_start(q):
         for d in range(1, C):
-            go(remote(part.at[q, at(SH * other(d), SH)], rsb.at[q, d - 1], rs_send.at[q, d], rs_recv.at[q, d], r, other(d)))
+            go(remote(part.at[q, at(SH * other(d), SH)], rsb.at[q, d - 1], rs_send.at[q], rs_recv.at[q], r, other(d)))
 
     def reduce_end(q):
         total = part[q, at(SH * c, SH), :]
+        landed((C - 1) * SH, rs_recv.at[q])
         for d in range(1, C):
-            landed(rsb.at[q, d - 1], rs_send.at[q, d], rs_recv.at[q, d])
             total = total + rsb[q, d - 1]
         ysh[q] = total
 
-    sizes = (2 * NB, 2 * NB, 3 * NB, NB)
+    sizes = (2 * NB, 2 * NB, NB, NB, 2 * NB)
 
     def sum_start(e):
         m = sizes[e] // C
         xb[e, x, 0:m, :] = pstack[e, at(m * c, m), :]
         for d in range(1, X):
             go(remote(
-                pstack.at[e, at(m * c, m)], xb.at[e, x, 0:m], px_send.at[e, d], px_recv.at[e, x],
+                pstack.at[e, at(m * c, m)], xb.at[e, x, 0:m], p_send.at[e], px_recv.at[e],
                 z * X + lax.rem(x + d, X), c,
             ))
 
     def sum_z(e):
         m = sizes[e] // C
-        for d in range(1, X):
-            k = lax.rem(x + d, X)
-            landed(xb.at[e, k, 0:m], px_send.at[e, d], px_recv.at[e, k])
+        landed((X - 1) * m, px_recv.at[e])
         zb[e, z, 0:m, :] = (xb[e, 0, 0:m, :] + xb[e, 1, 0:m, :]) + (xb[e, 2, 0:m, :] + xb[e, 3, 0:m, :])
         for d in range(1, Z):
             ref = zb.at[e, z, 0:m]
-            go(remote(ref, ref, pz_send.at[e, d], pz_recv.at[e, z], lax.rem(z + d, Z) * X + x, c))
+            go(remote(ref, ref, p_send.at[e], pz_recv.at[e], lax.rem(z + d, Z) * X + x, c))
 
     def sum_col(e):
         m = sizes[e] // C
-        for d in range(1, Z):
-            k = lax.rem(z + d, Z)
-            landed(zb.at[e, k, 0:m], pz_send.at[e, d], pz_recv.at[e, k])
+        landed((Z - 1) * m, pz_recv.at[e])
         total = zb[e, 0, 0:m, :]
         for k in range(1, Z):
             total = total + zb[e, k, 0:m, :]
         gsum[e, at(m * c, m), :] = total
         for d in range(1, C):
             ref = gsum.at[e, at(m * c, m)]
-            go(remote(ref, ref, pc_send.at[e, d], pc_recv.at[e, c], r, other(d)))
+            go(remote(ref, ref, p_send.at[e], pc_recv.at[e], r, other(d)))
 
     def sum_end(e):
-        m = sizes[e] // C
-        for d in range(1, C):
-            landed(gsum.at[e, at(m * other(d), m)], pc_send.at[e, d], pc_recv.at[e, other(d)])
+        landed((C - 1) * sizes[e] // C, pc_recv.at[e])
+
+    def drain():
+        def sent(ref, sem):
+            remote(ref, ref, sem, sem, r, c).wait_send()
+
+        for v in range(4):
+            sent(yp.at[pl.ds(0, (64 * HS + (C - 1) * SH) // 2)], v_send.at[v])
+        for q in range(2):
+            sent(cform.at[pl.ds(0, (C - 1) * SH)], rs_send.at[q])
+        for e in range(5):
+            sent(cform.at[pl.ds(0, (X + Z + C - 3) * sizes[e] // C)], p_send.at[e])
 
     inner = ((1,), (0,))
     both_last = ((1,), (1,))
@@ -339,7 +371,8 @@
     split_h()
     ring(PV, 4)
     sum_col(0)
-    ring_end(PV)
+    ring_last(PV)
+    ring_done(PV)
 
     @pl.loop(0, 8)
     def _(k):
@@ -351,7 +384,7 @@
     sum_end(0)
     scaled(0, 0)
     ring(CV, 1)
-    sweep(0, 4)
+    sweep(0, 6)
     reduce_end(0)
     distribute(YV, ysh.at[0])
     ring(CV, 2)
@@ -363,11 +396,12 @@
     pstack[1, 0:NB, :] = dot_tn(ypr[:, NB : 2 * NB], ypr[:, 0:NB])
     pstack[1, NB : 2 * NB, :] = dot_tn(cr[...], ypr[:, NB : 2 * NB])
     sum_start(1)
-    sweep(0, 6)
+    sweep(0, 4)
     ring(YV, 2)
     ring(CV, 4)
     sum_z(1)
     ring(YV, 3)
+    ring_last(CV)
     sum_col(1)
     ring(YV, 4)
     sum_end(1)
@@ -384,10 +418,10 @@
         p2r[0:NB, :] = jnp.zeros((NB, NB), F32)
 
     pstack[2, 0:NB, :] = dot_tn(p2r[...], p2r[...])
-    pstack[2, NB : 3 * NB, :] = dot_tn(ypr[...], p2r[...])
     sum_start(2)
-    ring_end(CV)
-    ring_end(YV)
+    ring_last(YV)
+    ring_done(CV)
+    ring_done(YV)
 
     @pl.loop(0, 8)
     def _(k):
@@ -402,6 +436,8 @@
     sum_z(2)
     times_h(1)
     reduce_start(1)
+    pstack[4] = dot_tn(ypr[...], p2r[...])
+    sum_start(4)
     sum_col(2)
     alpha1, beta1 = factors(ypr[:, NB : 2 * NB], ypr[:, 0:NB], k1, s1, d1)
     ab1[:, 0:NB] = alpha1
@@ -410,28 +446,32 @@
     distribute(UV, ysh.at[1])
     sum_end(2)
     scaled(1, 2)
-    sweep(1, 4)
+    sweep(1, 6)
     ring(UV, 1)
     wait_rows(UV)
     pstack[3, 0:NB, :] = dot_tn(p2r[...], ur[...])
     sum_start(3)
-    sweep(1, 6)
+    sum_z(4)
+    sweep(1, 5)
     ring(UV, 2)
     sum_z(3)
-    sweep(1, 6)
+    sweep(1, 5)
+    sum_col(4)
     ring(UV, 3)
     sum_col(3)
     k2, d2, e2 = inv[1], sc1[1], sc2[1]
-    t1, t2 = gsum[2, NB : 2 * NB, :], gsum[2, 2 * NB : 3 * NB, :]
+    pk2 = dot(p2r[...] * d2[0:1, :], k2)
+    alpha2 = -2.0 * pk2 * d2[0:1, :]
+    lhs_ref[0, :, 0:NB], lhs_ref[1, :, 0:NB] = halves(alpha2)
+    ring(UV, 4)
+    sum_end(4)
+    t1, t2 = gsum[4, 0:NB, :], gsum[4, NB : 2 * NB, :]
     kt2 = dot(k1, t2 * e1)
     ab[0:NB, :] = -2.0 * kt2 * e1
     ab[NB : 2 * NB, :] = dot(k1, 4.0 * dot(s1, kt2) - 2.0 * (t1 * e1)) * e1
-    pk2 = dot(p2r[...] * d2[0:1, :], k2)
-    alpha2 = -2.0 * pk2 * d2[0:1, :]
-    lhs_ref[0, :, 0:NB], lhs_ref[1, :, 0:NB] = halves(alpha2)
     abh[0], abh[1] = halves(ab1[...] + dot_nt(alpha2, ab[...]))
     y2 = ur[...] + dot(ypr[...], ab[...])
-    ring(UV, 4)
+    ring_last(UV)
 
     @pl.loop(0, 8)
     def _(k):
@@ -442,12 +482,11 @@
         )
 
     sum_end(3)
-    s2 = (gsum[3, 0:NB, :] + dot_tn(gsum[2, NB : 3 * NB, :], ab[...])) * d2 * e2
+    s2 = (gsum[3, 0:NB, :] + dot_tn(gsum[4], ab[...])) * d2 * e2
     beta2 = dot(4.0 * dot(pk2, s2) - 2.0 * (y2 * d2[0:1, :]), k2) * d2[0:1, :]
     lhs_ref[0, :, NB : 2 * NB], lhs_ref[1, :, NB : 2 * NB] = halves(beta2)
-    ring_end(UV)
-    for copy in started:
-        copy.wait_send()
+    ring_done(UV)
+    drain()
 
 
 def factors_kernel(hamiltonian):
@@ -477,10 +516,10 @@
             pltpu.VMEM((2, SH, NB), F32),
             pltpu.VMEM((2 * NB, NB), F32),
             pltpu.VMEM((2 * NB, NB), F32),
-            pltpu.VMEM((4, 3 * NB, NB), F32),
-            pltpu.VMEM((4, X, 3 * NB // C, NB), F32),
-            pltpu.VMEM((4, Z, 3 * NB // C, NB), F32),
-            pltpu.VMEM((4, 3 * NB, NB), F32),
+            pltpu.VMEM((5, 2 * NB, NB), F32),
+            pltpu.VMEM((5, X, 2 * NB // C, NB), F32),
+            pltpu.VMEM((5, Z, 2 * NB // C, NB), F32),
+            pltpu.VMEM((5, 2 * NB, NB), F32),
             pltpu.VMEM((2, NB, NB), F32),
             pltpu.VMEM((2, NB, NB), F32),
             pltpu.VMEM((2, NB, NB), F32),
@@ -489,11 +528,8 @@
             pltpu.VMEM((cols, 2 * NB), BF16),
             pltpu.VMEM((2 * NB, 2 * NB), BF16),
             pltpu.VMEM((2, rows, 2 * NB), BF16),
-            dma, dma((2,)), dma((2, C)), dma((2,)),
-            dma((4, C)), dma((4, C)), dma((4, 4)), dma((4, 4)),
-            dma((4, 2, 4, 4)), dma((4, 2, 4, 4)),
-            dma((2, C)), dma((2, C)),
-            dma((4, X)), dma((4, X)), dma((4, Z)), dma((4, Z)), dma((4, C)), dma((4, C)),
+            dma, dma((2,)), dma((2,)), dma((2,)), dma((4,)), dma((4,)), dma((4, 2)), dma((4, 2, 4, 2)), dma((4,)),
+            dma((2,)), dma((2,)), dma((5,)), dma((5,)), dma((5,)), dma((5,)),
         ],
         compiler_params=pltpu.CompilerParams(
             collective_id=0, has_side_effects=True, vmem_limit_bytes=36 * 1024 * 1024

time: 126 us -> 111 us (0.88)
  Pallas kernels: 126 us -> 110 us
    pallas_call x1, Pallas kernels: 121 us -> 105 us  [factors_kernel(): pl.pallas_call(kernel, out_shape=(pltpu.VMEM((rows, cols), F32), pltpu.VM...]
where the time goes in v4:
time: 111 us; the launch traced here: 110 us
  Pallas kernels  110 us (99%)
    pallas_call x1, Pallas kernels, factors_kernel(): pl.pallas_call(kernel, out_shape=(pltpu.VMEM((rows, cols), F32), pltpu.VM...  105 us
    pallas_call x1, Pallas kernels, update(): pl.pallas_call(update_kernel, grid=(cols // (2 * NB),), out_shape=jax.Sha...  5.24 us

profile of v4, /device:TPU:1, one launch (start us, length us, event | category | flops | bytes accessed | tf_op | source)
XLA Modules:
  0.0 110.3 jit_solution(3924393585372089642)
XLA Ops:
  0.0 105.1 %reflector_factors.1 = (f32[512,2048]{1,0:T(8,128)S(1)}, bf16[2,512,256]{2,1,0:T(8,128)(2,1)S(1)}, f32[2048,256]{1,0:T(8,128)S(1)}) custom-call(f32[512,2048]{1,0:T(8,128)} %h_hbm.1), custom_call_target="tpu_custom_call" | custom-call | tf_op jit(solution)/shard_map/reflector_factors/pallas_call | solution.py:496
  105.1 5.2 %apply_factors.1 = f32[512,2048]{1,0:T(8,128)} custom-call(f32[512,2048]{1,0:T(8,128)S(1)} %get-tuple-element.8.h_ref, bf16[2,512,256]{2,1,0:T(8,128)(2,1)S(1)} %get-tuple-element.9.lhs_ref, f32[2048,256]{1,0:T(8,128)S(1)} %get-tuple-element.10.up_ref), custom_call_target="tpu_custom_call" | custom-call | tf_op jit(solution)/shard_map/apply_factors/pallas_call | solution.py:553

commit v5 on v4

--- a/solution.py
+++ b/solution.py
@@ -89,8 +89,8 @@
 
 
 def kernel(
-    h_hbm, hv, lhs_ref, up,
-    sh, yp, cform, ypr, cr, ur, p2r, ab1, part, rsb, ysh, abt, ab,
+    h_hbm, hv, lhs_ref, up, rest,
+    sh, yp, cform, ypr, cr, ur, p2r, part, rsb, ysh, abt, ab,
     pstack, xb, zb, gsum, inv, sc1, sc2, hh, hl, vs, abts, abh,
     h_sem, loc_sem, sc_send, sc_recv, v_send, ra_recv, sp_recv, rp_recv, rx_recv,
     rs_send, rs_recv, p_send, px_recv, pz_recv, pc_recv,
@@ -267,7 +267,7 @@
             total = total + rsb[q, d - 1]
         ysh[q] = total
 
-    sizes = (2 * NB, 2 * NB, NB, NB, 2 * NB)
+    sizes = (NB, NB, NB, NB, 2 * NB, 2 * NB)
 
     def sum_start(e):
         m = sizes[e] // C
@@ -308,7 +308,7 @@
             sent(yp.at[pl.ds(0, (64 * HS + (C - 1) * SH) // 2)], v_send.at[v])
         for q in range(2):
             sent(cform.at[pl.ds(0, (C - 1) * SH)], rs_send.at[q])
-        for e in range(5):
+        for e in range(6):
             sent(cform.at[pl.ds(0, (X + Z + C - 3) * sizes[e] // C)], p_send.at[e])
 
     inner = ((1,), (0,))
@@ -347,8 +347,16 @@
         beta = dot(4.0 * dot(pk, s) - 2.0 * (y * d[0:1, :]), k) * d[0:1, :]
         return alpha, beta
 
+    def apply_panel1(first, last):
+        @pl.loop(first, last)
+        def _(k):
+            cols = pl.ds(pl.multiple_of(k * 2 * NB, 2 * NB), 2 * NB)
+            high, low = halves(yp[cols, :])
+            hv[:, cols] = hv[:, cols] + (
+                dot_b(abh[0], high, both_last) + (dot_b(abh[0], low, both_last) + dot_b(abh[1], high, both_last))
+            )
+
     finish_p = scatter(PV)
-    finish_c = scatter(CV)
     finish_p()
 
     @pl.when((r == 0) & (c < 2))
@@ -356,11 +364,11 @@
         sh[PV] = jnp.zeros((SH, NB), F32)
 
     distribute(PV, sh.at[PV])
+    finish_c = scatter(CV)
     ring(PV, 1)
     wait_rows(PV)
     p1 = ypr[:, NB : 2 * NB]
     pstack[0, 0:NB, :] = dot_tn(p1, p1)
-    pstack[0, NB : 2 * NB, :] = jnp.where(r == 1, ypr[0:NB, NB : 2 * NB], 0.0)
     sum_start(0)
     ring(PV, 2)
     sum_z(0)
@@ -372,6 +380,7 @@
     ring(PV, 4)
     sum_col(0)
     ring_last(PV)
+    ring(CV, 1)
     ring_done(PV)
 
     @pl.loop(0, 8)
@@ -381,33 +390,40 @@
 
     times_h(0)
     reduce_start(0)
+    ring(CV, 2)
     sum_end(0)
     scaled(0, 0)
-    ring(CV, 1)
-    sweep(0, 6)
+    sweep(0, 3)
+    ring(CV, 3)
+    wait_rows(CV)
+    pstack[5, 0:NB, :] = dot_tn(cr[...], ypr[:, NB : 2 * NB])
+    pstack[5, NB : 2 * NB, :] = jnp.where(r == 1, ypr[0:NB, NB : 2 * NB], 0.0)
+    sum_start(5)
     reduce_end(0)
     distribute(YV, ysh.at[0])
-    ring(CV, 2)
-    sweep(0, 6)
+    ring(CV, 4)
+    sweep(0, 4)
+    sum_z(5)
+    ring_last(CV)
     ring(YV, 1)
-    ring(CV, 3)
-    wait_rows(CV)
     wait_rows(YV)
     pstack[1, 0:NB, :] = dot_tn(ypr[:, NB : 2 * NB], ypr[:, 0:NB])
-    pstack[1, NB : 2 * NB, :] = dot_tn(cr[...], ypr[:, NB : 2 * NB])
     sum_start(1)
-    sweep(0, 4)
+    sweep(0, 3)
     ring(YV, 2)
-    ring(CV, 4)
     sum_z(1)
+    sweep(0, 3)
+    sum_col(5)
     ring(YV, 3)
-    ring_last(CV)
+    sweep(0, 3)
     sum_col(1)
     ring(YV, 4)
+    sum_end(5)
+    ring_last(YV)
     sum_end(1)
     k1, d1, e1 = inv[0], sc1[0], sc2[0]
     s1 = gsum[1, 0:NB, :] * d1 * e1
-    alpha_b, beta_b = factors(gsum[0, NB : 2 * NB, :], gsum[1, NB : 2 * NB, :], k1, s1, d1)
+    alpha_b, beta_b = factors(gsum[5, NB : 2 * NB, :], gsum[5, 0:NB, :], k1, s1, d1)
     abt[0:NB, :] = alpha_b.T
     abt[NB : 2 * NB, :] = beta_b.T
     abts[:, 0:NB], abts[:, NB : 2 * NB] = halves(abt[...])
@@ -419,7 +435,6 @@
 
     pstack[2, 0:NB, :] = dot_tn(p2r[...], p2r[...])
     sum_start(2)
-    ring_last(YV)
     ring_done(CV)
     ring_done(YV)
 
@@ -438,49 +453,50 @@
     reduce_start(1)
     pstack[4] = dot_tn(ypr[...], p2r[...])
     sum_start(4)
+    alpha1, beta1 = factors(ypr[:, NB : 2 * NB], ypr[:, 0:NB], k1, s1, d1)
+    abh[0, :, 0:NB], abh[1, :, 0:NB] = halves(alpha1)
+    abh[0, :, NB : 2 * NB], abh[1, :, NB : 2 * NB] = halves(beta1)
     sum_col(2)
-    alpha1, beta1 = factors(ypr[:, NB : 2 * NB], ypr[:, 0:NB], k1, s1, d1)
-    ab1[:, 0:NB] = alpha1
-    ab1[:, NB : 2 * NB] = beta1
+    apply_panel1(0, 4)
     reduce_end(1)
     distribute(UV, ysh.at[1])
+    sum_z(4)
     sum_end(2)
     scaled(1, 2)
-    sweep(1, 6)
+    sweep(1, 8)
     ring(UV, 1)
     wait_rows(UV)
     pstack[3, 0:NB, :] = dot_tn(p2r[...], ur[...])
     sum_start(3)
-    sum_z(4)
-    sweep(1, 5)
+    sweep(1, 3)
     ring(UV, 2)
     sum_z(3)
     sweep(1, 5)
+    ring(UV, 3)
     sum_col(4)
-    ring(UV, 3)
-    sum_col(3)
     k2, d2, e2 = inv[1], sc1[1], sc2[1]
     pk2 = dot(p2r[...] * d2[0:1, :], k2)
     alpha2 = -2.0 * pk2 * d2[0:1, :]
     lhs_ref[0, :, 0:NB], lhs_ref[1, :, 0:NB] = halves(alpha2)
+    apply_panel1(4, 6)
     ring(UV, 4)
+    sum_col(3)
+    apply_panel1(6, 8)
     sum_end(4)
     t1, t2 = gsum[4, 0:NB, :], gsum[4, NB : 2 * NB, :]
     kt2 = dot(k1, t2 * e1)
     ab[0:NB, :] = -2.0 * kt2 * e1
     ab[NB : 2 * NB, :] = dot(k1, 4.0 * dot(s1, kt2) - 2.0 * (t1 * e1)) * e1
-    abh[0], abh[1] = halves(ab1[...] + dot_nt(alpha2, ab[...]))
-    y2 = ur[...] + dot(ypr[...], ab[...])
+    abts[:, 0:NB], abts[:, NB : 2 * NB] = halves(ab[...])
     ring_last(UV)
 
     @pl.loop(0, 8)
     def _(k):
-        cols = pl.ds(pl.multiple_of(k * 2 * NB, 2 * NB), 2 * NB)
-        high, low = halves(yp[cols, :])
-        hv[:, cols] = hv[:, cols] + (
-            dot_b(abh[0], high, both_last) + (dot_b(abh[0], low, both_last) + dot_b(abh[1], high, both_last))
-        )
-
+        rows = pl.ds(pl.multiple_of(k * 2 * NB, 2 * NB), 2 * NB)
+        high, low = halves(yp[rows, :])
+        rest[rows, :] = fold(dot_b(high, abts[...], inner) + dot_b(low, abts[...], inner))
+
+    y2 = ur[...] + dot(ypr[...], ab[...])
     sum_end(3)
     s2 = (gsum[3, 0:NB, :] + dot_tn(gsum[4], ab[...])) * d2 * e2
     beta2 = dot(4.0 * dot(pk2, s2) - 2.0 * (y2 * d2[0:1, :]), k2) * d2[0:1, :]
@@ -499,9 +515,10 @@
             pltpu.VMEM((rows, cols), F32),
             pltpu.VMEM((2, rows, 2 * NB), BF16),
             pltpu.VMEM((cols, 2 * NB), F32),
+            pltpu.VMEM((cols, NB), F32),
         ),
         in_specs=[pl.BlockSpec(memory_space=pltpu.HBM)],
-        out_specs=(vmem, vmem, vmem),
+        out_specs=(vmem, vmem, vmem, vmem),
         scratch_shapes=[
             pltpu.VMEM((2, SH, NB), F32),
             pltpu.VMEM((cols, 2 * NB), F32),
@@ -510,16 +527,15 @@
             pltpu.VMEM((rows, NB), F32),
             pltpu.VMEM((rows, NB), F32),
             pltpu.VMEM((rows, NB), F32),
-            pltpu.VMEM((rows, 2 * NB), F32),
             pltpu.VMEM((2, rows, NB), F32),
             pltpu.VMEM((2, C - 1, SH, NB), F32),
             pltpu.VMEM((2, SH, NB), F32),
             pltpu.VMEM((2 * NB, NB), F32),
             pltpu.VMEM((2 * NB, NB), F32),
-            pltpu.VMEM((5, 2 * NB, NB), F32),
-            pltpu.VMEM((5, X, 2 * NB // C, NB), F32),
-            pltpu.VMEM((5, Z, 2 * NB // C, NB), F32),
-            pltpu.VMEM((5, 2 * NB, NB), F32),
+            pltpu.VMEM((6, 2 * NB, NB), F32),
+            pltpu.VMEM((6, X, 2 * NB // C, NB), F32),
+            pltpu.VMEM((6, Z, 2 * NB // C, NB), F32),
+            pltpu.VMEM((6, 2 * NB, NB), F32),
             pltpu.VMEM((2, NB, NB), F32),
             pltpu.VMEM((2, NB, NB), F32),
             pltpu.VMEM((2, NB, NB), F32),
@@ -529,7 +545,7 @@
             pltpu.VMEM((2 * NB, 2 * NB), BF16),
             pltpu.VMEM((2, rows, 2 * NB), BF16),
             dma, dma((2,)), dma((2,)), dma((2,)), dma((4,)), dma((4,)), dma((4, 2)), dma((4, 2, 4, 2)), dma((4,)),
-            dma((2,)), dma((2,)), dma((5,)), dma((5,)), dma((5,)), dma((5,)),
+            dma((2,)), dma((2,)), dma((6,)), dma((6,)), dma((6,)), dma((6,)),
         ],
         compiler_params=pltpu.CompilerParams(
             collective_id=0, has_side_effects=True, vmem_limit_bytes=36 * 1024 * 1024
@@ -538,27 +554,30 @@
     )(hamiltonian)
 
 
-def update_kernel(h_ref, lhs_ref, up_ref, out_ref):
+def update_kernel(h_ref, lhs_ref, up_ref, rest_ref, out_ref):
     cols = pl.ds(pl.multiple_of(pl.program_id(0) * 2 * NB, 2 * NB), 2 * NB)
-    high, low = halves(up_ref[cols, :])
+    y_high, y_low = halves(up_ref[cols, 0:NB] + rest_ref[cols, :])
+    p_high, p_low = halves(up_ref[cols, NB : 2 * NB])
+    high = jnp.concatenate([y_high, p_high], axis=1)
+    low = jnp.concatenate([y_low, p_low], axis=1)
     last = ((1,), (1,))
     out_ref[...] = h_ref[:, cols] + (
         dot_b(lhs_ref[0], high, last) + (dot_b(lhs_ref[0], low, last) + dot_b(lhs_ref[1], high, last))
     )
 
 
-def update(partly, lhs, up):
+def update(partly, lhs, up, rest):
     rows, cols = partly.shape
     vmem = pl.BlockSpec(memory_space=pltpu.VMEM)
     return pl.pallas_call(
         update_kernel,
         grid=(cols // (2 * NB),),
         out_shape=jax.ShapeDtypeStruct((rows, cols), F32),
-        in_specs=[vmem, vmem, vmem],
+        in_specs=[vmem, vmem, vmem, vmem],
         out_specs=pl.BlockSpec((rows, 2 * NB), lambda i: (0, i)),
         compiler_params=pltpu.CompilerParams(vmem_limit_bytes=20 * 1024 * 1024),
         name="apply_factors",
-    )(partly, lhs, up)
+    )(partly, lhs, up, rest)
 
 
 def body(hamiltonian):

time: 111 us -> 106 us (0.955)
  Pallas kernels: 110 us -> 105 us
    pallas_call x1, Pallas kernels: 105 us -> 100 us  [factors_kernel(): pl.pallas_call(kernel, out_shape=(pltpu.VMEM((rows, cols), F32), pltpu.VM...]
where the time goes in v5:
time: 106 us; the launch traced here: 105 us
  Pallas kernels  105 us (99%)
    pallas_call x1, Pallas kernels, factors_kernel(): pl.pallas_call(kernel, out_shape=(pltpu.VMEM((rows, cols), F32), pltpu.VM...  100 us
    pallas_call x1, Pallas kernels, update(): pl.pallas_call(update_kernel, grid=(cols // (2 * NB),), out_shape=jax.Sha...  5.25 us

profile of v5, /device:TPU:1, one launch (start us, length us, event | category | flops | bytes accessed | tf_op | source)
XLA Modules:
  0.0 105.3 jit_solution(8582037328723647719)
XLA Ops:
  0.0 100.0 %reflector_factors.1 = (f32[512,2048]{1,0:T(8,128)S(1)}, bf16[2,512,256]{2,1,0:T(8,128)(2,1)S(1)}, f32[2048,256]{1,0:T(8,128)S(1)}, f32[2048,128]{1,0:T(8,128)S(1)}) custom-call(f32[512,2048]{1,0:T(8,128)} %h_hbm.1), custom_call_target="tpu_custom_call" | custom-call | tf_op jit(solution)/shard_map/reflector_factors/pallas_call | solution.py:512
  100.0 5.2 %apply_factors.1 = f32[512,2048]{1,0:T(8,128)} custom-call(f32[512,2048]{1,0:T(8,128)S(1)} %get-tuple-element.9.h_ref, bf16[2,512,256]{2,1,0:T(8,128)(2,1)S(1)} %get-tuple-element.10.lhs_ref, f32[2048,256]{1,0:T(8,128)S(1)} %get-tuple-element.11.up_ref, f32[2048,128]{1,0:T(8,128)S(1)} %get-tuple-element.12.rest_ref), custom_call_target="tpu_custom_call" | custom-call | tf_op jit(solution)/shard_map/apply_factors/pallas_call | solution.py:572

commit v6 on v5

--- a/solution.py
+++ b/solution.py
@@ -85,13 +85,13 @@
         a = jnp.concatenate([a[1:], a[:1]], axis=0)
         return pltpu.roll(a, NB - 8, 2)
 
-    return lax.fori_loop(0, groups, group, a.reshape(NB // 8, 8, NB)).reshape(NB, NB)
+    return lax.fori_loop(0, groups, group, a.reshape(NB // 8, 8, NB), unroll=True).reshape(NB, NB)
 
 
 def kernel(
-    h_hbm, hv, lhs_ref, up, rest,
+    h_hbm, hv, lhs_ref, up, rest, vs,
     sh, yp, cform, ypr, cr, ur, p2r, part, rsb, ysh, abt, ab,
-    pstack, xb, zb, gsum, inv, sc1, sc2, hh, hl, vs, abts, abh,
+    pstack, xb, zb, gsum, inv, sc1, sc2, hh, hl, yh, yl, abts, abh,
     h_sem, loc_sem, sc_send, sc_recv, v_send, ra_recv, sp_recv, rp_recv, rx_recv,
     rs_send, rs_recv, p_send, px_recv, pz_recv, pc_recv,
 ):
@@ -150,7 +150,7 @@
             return cform.at[rows]
         if v == PV:
             return yp.at[rows, NB : 2 * NB]
-        return (up if v == UV else yp).at[rows, 0:NB]
+        return up.at[rows] if v == UV else yp.at[rows, 0:NB]
 
     def row(v, rows):
         if v == PV:
@@ -238,7 +238,7 @@
                 for i in pair:
                     pass_x(v, i, z)
                 continue
-            for up_way in (True, False):
+            for up_way in (g == 0, g != 0):
                 landed(2 * HS, rp_recv.at[v, 0 if up_way else 1, s - 2, g])
                 if s < 4 or up_way == (g == 0):
                     for i in pair:
@@ -351,11 +351,17 @@
         @pl.loop(first, last)
         def _(k):
             cols = pl.ds(pl.multiple_of(k * 2 * NB, 2 * NB), 2 * NB)
-            high, low = halves(yp[cols, :])
+            high, low = yh[cols, :], yl[cols, :]
             hv[:, cols] = hv[:, cols] + (
                 dot_b(abh[0], high, both_last) + (dot_b(abh[0], low, both_last) + dot_b(abh[1], high, both_last))
             )
 
+    def rest_of_y2(first, last):
+        @pl.loop(first, last)
+        def _(k):
+            rows = pl.ds(pl.multiple_of(k * 2 * NB, 2 * NB), 2 * NB)
+            rest[rows, :] = fold(dot_b(yh[rows, :], abts[...], inner) + dot_b(yl[rows, :], abts[...], inner))
+
     finish_p = scatter(PV)
     finish_p()
 
@@ -366,19 +372,18 @@
     distribute(PV, sh.at[PV])
     finish_c = scatter(CV)
     ring(PV, 1)
+    ring(PV, 2)
     wait_rows(PV)
     p1 = ypr[:, NB : 2 * NB]
     pstack[0, 0:NB, :] = dot_tn(p1, p1)
     sum_start(0)
-    ring(PV, 2)
-    sum_z(0)
     ring(PV, 3)
     finish_c()
     distribute(CV, sh.at[CV])
     copy_h.wait()
     split_h()
     ring(PV, 4)
-    sum_col(0)
+    sum_z(0)
     ring_last(PV)
     ring(CV, 1)
     ring_done(PV)
@@ -386,33 +391,35 @@
     @pl.loop(0, 8)
     def _(k):
         rows = pl.ds(pl.multiple_of(k * 2 * NB, 2 * NB), 2 * NB)
-        vs[rows, 0:NB], vs[rows, NB : 2 * NB] = halves(yp[rows, NB : 2 * NB])
+        high, low = halves(yp[rows, NB : 2 * NB])
+        vs[rows, 0:NB], vs[rows, NB : 2 * NB] = high, low
+        yh[rows, NB : 2 * NB], yl[rows, NB : 2 * NB] = high, low
 
     times_h(0)
     reduce_start(0)
+    sum_col(0)
     ring(CV, 2)
-    sum_end(0)
-    scaled(0, 0)
-    sweep(0, 3)
-    ring(CV, 3)
     wait_rows(CV)
     pstack[5, 0:NB, :] = dot_tn(cr[...], ypr[:, NB : 2 * NB])
     pstack[5, NB : 2 * NB, :] = jnp.where(r == 1, ypr[0:NB, NB : 2 * NB], 0.0)
     sum_start(5)
+    ring(CV, 3)
     reduce_end(0)
     distribute(YV, ysh.at[0])
     ring(CV, 4)
-    sweep(0, 4)
+    sum_end(0)
+    scaled(0, 0)
+    sweep(0, 5)
     sum_z(5)
     ring_last(CV)
     ring(YV, 1)
     wait_rows(YV)
     pstack[1, 0:NB, :] = dot_tn(ypr[:, NB : 2 * NB], ypr[:, 0:NB])
     sum_start(1)
-    sweep(0, 3)
+    sweep(0, 4)
     ring(YV, 2)
     sum_z(1)
-    sweep(0, 3)
+    sweep(0, 4)
     sum_col(5)
     ring(YV, 3)
     sweep(0, 3)
@@ -441,62 +448,55 @@
     @pl.loop(0, 8)
     def _(k):
         rows = pl.ds(pl.multiple_of(k * 2 * NB, 2 * NB), 2 * NB)
-        high, low = halves(yp[rows, :])
-        value = cform[rows, :] + fold(dot_b(high, abts[...], inner) + dot_b(low, abts[...], inner))
+        yh[rows, 0:NB], yl[rows, 0:NB] = halves(yp[rows, 0:NB])
+        value = cform[rows, :] + fold(dot_b(yh[rows, :], abts[...], inner) + dot_b(yl[rows, :], abts[...], inner))
         sub = lax.broadcasted_iota(jnp.int32, (2 * NB, NB), 0)
         value = jnp.where((sub < NB) & (k == 0) & (c < 2), 0.0, value)
-        up[rows, NB : 2 * NB] = value
         vs[rows, 0:NB], vs[rows, NB : 2 * NB] = halves(value)
 
-    sum_z(2)
     times_h(1)
     reduce_start(1)
+    sum_z(2)
     pstack[4] = dot_tn(ypr[...], p2r[...])
     sum_start(4)
     alpha1, beta1 = factors(ypr[:, NB : 2 * NB], ypr[:, 0:NB], k1, s1, d1)
     abh[0, :, 0:NB], abh[1, :, 0:NB] = halves(alpha1)
     abh[0, :, NB : 2 * NB], abh[1, :, NB : 2 * NB] = halves(beta1)
+    apply_panel1(0, 4)
     sum_col(2)
-    apply_panel1(0, 4)
     reduce_end(1)
     distribute(UV, ysh.at[1])
     sum_z(4)
+    apply_panel1(4, 6)
     sum_end(2)
     scaled(1, 2)
-    sweep(1, 8)
+    sweep(1, 6)
     ring(UV, 1)
     wait_rows(UV)
     pstack[3, 0:NB, :] = dot_tn(p2r[...], ur[...])
     sum_start(3)
-    sweep(1, 3)
+    sum_col(4)
+    sweep(1, 4)
     ring(UV, 2)
     sum_z(3)
-    sweep(1, 5)
+    sweep(1, 6)
     ring(UV, 3)
-    sum_col(4)
-    k2, d2, e2 = inv[1], sc1[1], sc2[1]
-    pk2 = dot(p2r[...] * d2[0:1, :], k2)
-    alpha2 = -2.0 * pk2 * d2[0:1, :]
-    lhs_ref[0, :, 0:NB], lhs_ref[1, :, 0:NB] = halves(alpha2)
-    apply_panel1(4, 6)
-    ring(UV, 4)
-    sum_col(3)
-    apply_panel1(6, 8)
     sum_end(4)
     t1, t2 = gsum[4, 0:NB, :], gsum[4, NB : 2 * NB, :]
     kt2 = dot(k1, t2 * e1)
     ab[0:NB, :] = -2.0 * kt2 * e1
     ab[NB : 2 * NB, :] = dot(k1, 4.0 * dot(s1, kt2) - 2.0 * (t1 * e1)) * e1
     abts[:, 0:NB], abts[:, NB : 2 * NB] = halves(ab[...])
+    rest_of_y2(0, 4)
+    sum_col(3)
+    ring(UV, 4)
+    rest_of_y2(4, 8)
+    k2, d2, e2 = inv[1], sc1[1], sc2[1]
+    pk2 = dot(p2r[...] * d2[0:1, :], k2)
+    lhs_ref[0, :, 0:NB], lhs_ref[1, :, 0:NB] = halves(-2.0 * pk2 * d2[0:1, :])
     ring_last(UV)
-
-    @pl.loop(0, 8)
-    def _(k):
-        rows = pl.ds(pl.multiple_of(k * 2 * NB, 2 * NB), 2 * NB)
-        high, low = halves(yp[rows, :])
-        rest[rows, :] = fold(dot_b(high, abts[...], inner) + dot_b(low, abts[...], inner))
-
     y2 = ur[...] + dot(ypr[...], ab[...])
+    apply_panel1(6, 8)
     sum_end(3)
     s2 = (gsum[3, 0:NB, :] + dot_tn(gsum[4], ab[...])) * d2 * e2
     beta2 = dot(4.0 * dot(pk2, s2) - 2.0 * (y2 * d2[0:1, :]), k2) * d2[0:1, :]
@@ -514,11 +514,12 @@
         out_shape=(
             pltpu.VMEM((rows, cols), F32),
             pltpu.VMEM((2, rows, 2 * NB), BF16),
-            pltpu.VMEM((cols, 2 * NB), F32),
             pltpu.VMEM((cols, NB), F32),
+            pltpu.VMEM((cols, NB), F32),
+            pltpu.VMEM((cols, 2 * NB), BF16),
         ),
         in_specs=[pl.BlockSpec(memory_space=pltpu.HBM)],
-        out_specs=(vmem, vmem, vmem, vmem),
+        out_specs=(vmem, vmem, vmem, vmem, vmem),
         scratch_shapes=[
             pltpu.VMEM((2, SH, NB), F32),
             pltpu.VMEM((cols, 2 * NB), F32),
@@ -542,6 +543,7 @@
             pltpu.VMEM((rows, cols), BF16),
             pltpu.VMEM((rows, cols), BF16),
             pltpu.VMEM((cols, 2 * NB), BF16),
+            pltpu.VMEM((cols, 2 * NB), BF16),
             pltpu.VMEM((2 * NB, 2 * NB), BF16),
             pltpu.VMEM((2, rows, 2 * NB), BF16),
             dma, dma((2,)), dma((2,)), dma((2,)), dma((4,)), dma((4,)), dma((4, 2)), dma((4, 2, 4, 2)), dma((4,)),
@@ -554,30 +556,29 @@
     )(hamiltonian)
 
 
-def update_kernel(h_ref, lhs_ref, up_ref, rest_ref, out_ref):
+def update_kernel(h_ref, lhs_ref, u_ref, rest_ref, vs_ref, out_ref):
     cols = pl.ds(pl.multiple_of(pl.program_id(0) * 2 * NB, 2 * NB), 2 * NB)
-    y_high, y_low = halves(up_ref[cols, 0:NB] + rest_ref[cols, :])
-    p_high, p_low = halves(up_ref[cols, NB : 2 * NB])
-    high = jnp.concatenate([y_high, p_high], axis=1)
-    low = jnp.concatenate([y_low, p_low], axis=1)
+    y_high, y_low = halves(u_ref[cols, :] + rest_ref[cols, :])
+    high = jnp.concatenate([y_high, vs_ref[cols, 0:NB]], axis=1)
+    low = jnp.concatenate([y_low, vs_ref[cols, NB : 2 * NB]], axis=1)
     last = ((1,), (1,))
     out_ref[...] = h_ref[:, cols] + (
         dot_b(lhs_ref[0], high, last) + (dot_b(lhs_ref[0], low, last) + dot_b(lhs_ref[1], high, last))
     )
 
 
-def update(partly, lhs, up, rest):
+def update(partly, lhs, u, rest, halves_of_p2):
     rows, cols = partly.shape
     vmem = pl.BlockSpec(memory_space=pltpu.VMEM)
     return pl.pallas_call(
         update_kernel,
         grid=(cols // (2 * NB),),
         out_shape=jax.ShapeDtypeStruct((rows, cols), F32),
-        in_specs=[vmem, vmem, vmem, vmem],
+        in_specs=[vmem, vmem, vmem, vmem, vmem],
         out_specs=pl.BlockSpec((rows, 2 * NB), lambda i: (0, i)),
         compiler_params=pltpu.CompilerParams(vmem_limit_bytes=20 * 1024 * 1024),
         name="apply_factors",
-    )(partly, lhs, up, rest)
+    )(partly, lhs, u, rest, halves_of_p2)
 
 
 def body(hamiltonian):

time: 106 us -> 104 us (0.981)
  Pallas kernels: 105 us -> 103 us
    pallas_call x1, Pallas kernels: 100 us -> 97.8 us  [factors_kernel(): pl.pallas_call(kernel, out_shape=(pltpu.VMEM((rows, cols), F32), pltpu.VM...]
where the time goes in v6:
time: 104 us; the launch traced here: 103 us
  Pallas kernels  103 us (99%)
    pallas_call x1, Pallas kernels, factors_kernel(): pl.pallas_call(kernel, out_shape=(pltpu.VMEM((rows, cols), F32), pltpu.VM...  97.8 us
    pallas_call x1, Pallas kernels, update(): pl.pallas_call(update_kernel, grid=(cols // (2 * NB),), out_shape=jax.Sha...  5.25 us

profile of v6, /device:TPU:1, one launch (start us, length us, event | category | flops | bytes accessed | tf_op | source)
XLA Modules:
  0.0 103.0 jit_solution(16655714736763280726)
XLA Ops:
  0.0 97.8 %reflector_factors.1 = (f32[512,2048]{1,0:T(8,128)S(1)}, bf16[2,512,256]{2,1,0:T(8,128)(2,1)S(1)}, f32[2048,128]{1,0:T(8,128)S(1)}, f32[2048,128]{1,0:T(8,128)S(1)}, bf16[2048,256]{1,0:T(8,128)(2,1)S(1)}) custom-call(f32[512,2048]{1,0:T(8,128)} %h_hbm.1), custom_call_target="tpu_custom_call" | custom-call | tf_op jit(solution)/shard_map/reflector_factors/pallas_call | solution.py:512
  97.8 5.2 %apply_factors.1 = f32[512,2048]{1,0:T(8,128)} custom-call(f32[512,2048]{1,0:T(8,128)S(1)} %get-tuple-element.10.h_ref, bf16[2,512,256]{2,1,0:T(8,128)(2,1)S(1)} %get-tuple-element.11.lhs_ref, f32[2048,128]{1,0:T(8,128)S(1)} %get-tuple-element.12.u_ref, f32[2048,128]{1,0:T(8,128)S(1)} %get-tuple-element.13.rest_ref, ...), custom_call_target="tpu_custom_call" | custom-call | tf_op jit(solution)/shard_map/apply_factors/pallas_call | solution.py:573

commit v7 on v6

--- a/solution.py
+++ b/solution.py
@@ -557,7 +557,7 @@
 
 
 def update_kernel(h_ref, lhs_ref, u_ref, rest_ref, vs_ref, out_ref):
-    cols = pl.ds(pl.multiple_of(pl.program_id(0) * 2 * NB, 2 * NB), 2 * NB)
+    cols = pl.ds(pl.multiple_of(pl.program_id(0) * 4 * NB, 4 * NB), 4 * NB)
     y_high, y_low = halves(u_ref[cols, :] + rest_ref[cols, :])
     high = jnp.concatenate([y_high, vs_ref[cols, 0:NB]], axis=1)
     low = jnp.concatenate([y_low, vs_ref[cols, NB : 2 * NB]], axis=1)
@@ -572,10 +572,10 @@
     vmem = pl.BlockSpec(memory_space=pltpu.VMEM)
     return pl.pallas_call(
         update_kernel,
-        grid=(cols // (2 * NB),),
+        grid=(cols // (4 * NB),),
         out_shape=jax.ShapeDtypeStruct((rows, cols), F32),
         in_specs=[vmem, vmem, vmem, vmem, vmem],
-        out_specs=pl.BlockSpec((rows, 2 * NB), lambda i: (0, i)),
+        out_specs=pl.BlockSpec((rows, 4 * NB), lambda i: (0, i)),
         compiler_params=pltpu.CompilerParams(vmem_limit_bytes=20 * 1024 * 1024),
         name="apply_factors",
     )(partly, lhs, u, rest, halves_of_p2)

time: 104 us -> 102 us (0.981)
    pallas_call x1, Pallas kernels: 5.25 us -> 3.83 us  [update(): pl.pallas_call(update_kernel, grid=(cols // (4 * NB),), out_shape=jax.Sha...]
where the time goes in v7:
time: 102 us
  Pallas kernels  102 us (100%)
    pallas_call x1, Pallas kernels, factors_kernel(): pl.pallas_call(kernel, out_shape=(pltpu.VMEM((rows, cols), F32), pltpu.VM...  97.8 us
    pallas_call x1, Pallas kernels, update(): pl.pallas_call(update_kernel, grid=(cols // (4 * NB),), out_shape=jax.Sha...  3.83 us

profile of v7, /device:TPU:1, one launch (start us, length us, event | category | flops | bytes accessed | tf_op | source)
XLA Modules:
  0.0 101.6 jit_solution(11500466690079318530)
XLA Ops:
  0.0 97.8 %reflector_factors.1 = (f32[512,2048]{1,0:T(8,128)S(1)}, bf16[2,512,256]{2,1,0:T(8,128)(2,1)S(1)}, f32[2048,128]{1,0:T(8,128)S(1)}, f32[2048,128]{1,0:T(8,128)S(1)}, bf16[2048,256]{1,0:T(8,128)(2,1)S(1)}) custom-call(f32[512,2048]{1,0:T(8,128)} %h_hbm.1), custom_call_target="tpu_custom_call" | custom-call | tf_op jit(solution)/shard_map/reflector_factors/pallas_call | solution.py:512
  97.8 3.8 %apply_factors.1 = f32[512,2048]{1,0:T(8,128)} custom-call(f32[512,2048]{1,0:T(8,128)S(1)} %get-tuple-element.10.h_ref, bf16[2,512,256]{2,1,0:T(8,128)(2,1)S(1)} %get-tuple-element.11.lhs_ref, f32[2048,128]{1,0:T(8,128)S(1)} %get-tuple-element.12.u_ref, f32[2048,128]{1,0:T(8,128)S(1)} %get-tuple-element.13.rest_ref, ...), custom_call_target="tpu_custom_call" | custom-call | tf_op jit(solution)/shard_map/apply_factors/pallas_call | solution.py:573
